TPU v7x, 256 devices: a whole 4x4x8 slice. The times are simulated.
256 devices in a mesh: rec: 32 (over x, y, core), tile: 8 (over z).
Axes of the slice: x: 4, y: 4, z: 8, core: 2. Of those that a mesh axis runs over, the one named last changes fastest.
Arguments:
- deviation: float32 [64, 64, 1024], P(None, 'rec', 'tile'), may hold values from -6 to 6
- footprint: bfloat16 [8192, 8, 2, 8, 8, 128], P('rec', 'tile'), may hold values from -0.046875 to 0.046875
- tile_list: int32 [8192, 8, 2], P('rec', 'tile'), may hold values from -1 to 7, as said below
- offset: int32 [8192], P('rec'), may hold values from 0 to 56
- observed: float32 [8192], P('rec'), may hold values from -10 to 10
- obs_group: int32 [8192], P('rec'), may hold values from 0 to 3
- group_var: float32 [4], replicated, may hold values from 0.5 to 4
- inv_time: float32 [64, 64], replicated, as said below
- inv_lat: float32 [64, 64], replicated, as said below
- inv_lon: float32 [1024, 1024], P('tile'), as said below
Outputs:
- gradient: float32 [64, 64, 1024], P(None, 'rec', 'tile')
- misfit: float32 [8192], P('rec')
Inputs may be any that keep to these rules, and one draw needn't show every extreme that they name: `tile_list`: each entry is a latitude tile of 8 rows in the slot's longitude strip, or -1 for an unused slot; the tiles named by one receptor in one strip are distinct. `inv_lon`: symmetric and diagonally dominant with a positive diagonal. `inv_lat`: symmetric and diagonally dominant with a positive diagonal. `inv_time`: symmetric and diagonally dominant with a positive diagonal.
All inputs are finite; a program needn't handle non-finite values.
Results may differ from a plain program's by a relative error of at most 0.0003.
Values sent between devices are 32-bit elements; how exact they have to be, the bound alone decides.
A program may use at most 128 MiB of HBM per device.

v0:
```python
import jax
import jax.numpy as jnp
from jax import lax
from jax.sharding import PartitionSpec as P


def copy_for_each(value, axis):
    length = lax.axis_size(axis)
    return lax.all_to_all(
        jnp.broadcast_to(value[None], (length, *value.shape)), axis, 0, 0, tiled=True
    )


def laid_out(tiles, dim):
    tiles = jnp.moveaxis(tiles, 0, dim)
    shape = tiles.shape
    return tiles.reshape(*shape[:dim], shape[dim] * shape[dim + 1], *shape[dim + 2 :])


def gather_directly(value, axis, dim):
    tiles = copy_for_each(value, axis)
    return laid_out(tiles, dim)


def of_everyone(value, axis):
    return copy_for_each(value, axis).sum(axis=0)


def in_blocks(value, dim, length):
    shape = value.shape
    tiles = value.reshape(*shape[:dim], length, shape[dim] // length, *shape[dim + 1 :])
    return jnp.moveaxis(tiles, dim, 0)


def sent_and_summed(value, axis, dim):
    length = lax.axis_size(axis)
    tiles = lax.all_to_all(in_blocks(value, dim, length), axis, 0, 0, tiled=True)
    return jnp.sum(tiles, axis=0)


def shards(
    deviation,
    footprint,
    tile_list,
    offset,
    observed,
    obs_group,
    group_var,
    inv_time,
    inv_lat,
    inv_lon,
):
    highest = lax.Precision.HIGHEST
    periods, lat_dev, lon_dev = deviation.shape
    receptors, _, slot_count, window, tile_rows, _ = footprint.shape
    lat_all = lat_dev * lax.axis_size("rec")
    tiles_y = lat_all // tile_rows
    row_start = lax.axis_index("rec") * lat_dev
    strip_field = gather_directly(deviation, "rec", 1)
    flux_table = strip_field.reshape(periods * tiles_y, tile_rows * lon_dev)
    chosen = tile_list[:, 0, :]
    active = (chosen >= 0).astype(jnp.float32)
    starts = offset[:, None] + jnp.arange(window, dtype=jnp.int32)[None, :]
    row_index = (starts[:, None, :] * tiles_y + jnp.maximum(chosen, 0)[:, :, None]).reshape(-1)
    blocks = footprint.reshape(receptors * slot_count * window, tile_rows * lon_dev)
    picked = jnp.take(flux_table, row_index, axis=0)
    products = jnp.sum(blocks.astype(jnp.float32) * picked, axis=1).reshape(
        receptors, slot_count, window
    )
    partial_pred = jnp.sum(jnp.sum(products, axis=2) * active, axis=1)
    predicted = of_everyone(partial_pred, "tile")
    matches = obs_group[:, None] == jnp.arange(group_var.shape[0], dtype=jnp.int32)[None, :]
    variance = jnp.sum(jnp.where(matches, group_var[None, :], 0.0), axis=1)
    misfit = (predicted - observed) / variance
    slot_weight = jnp.broadcast_to(
        (misfit[:, None] * active)[:, :, None], (receptors, slot_count, window)
    )
    contrib = blocks.astype(jnp.float32) * slot_weight.reshape(-1, 1)
    partial_adj = jax.ops.segment_sum(contrib, row_index, num_segments=periods * tiles_y)
    partial_adj = partial_adj.reshape(periods, lat_all, lon_dev)
    own_lat = lax.dynamic_slice_in_dim(inv_lat, row_start, lat_dev, 0)
    lat_done = jnp.einsum("an,pnm->pam", own_lat, strip_field, precision=highest)
    lon_done = jnp.einsum(
        "pam,cm->pac",
        lax.all_gather(lat_done, "tile", axis=2, tiled=True),
        inv_lon,
        precision=highest,
    )
    time_done = jnp.einsum("qp,pam->qam", inv_time, lon_done, precision=highest)
    adjoint_own = sent_and_summed(partial_adj, "rec", 1)
    gradient = time_done + adjoint_own
    return (gradient, misfit)


def solution(mesh):
    return jax.shard_map(
        shards,
        mesh=mesh,
        in_specs=(
            P(None, "rec", "tile"),
            P("rec", "tile", None, None, None, None),
            P("rec", "tile", None),
            P("rec"),
            P("rec"),
            P("rec"),
            P(),
            P(),
            P(),
            P("tile", None),
        ),
        out_specs=(P(None, "rec", "tile"), P("rec")),
        check_vma=False,
    )
```

profile of v0, /device:TPU:1, one launch (start us, length us, event | category | flops | bytes accessed | tf_op | source)
XLA Modules:
  0.0 184.7 jit_solution(13057695678469183099)
XLA Ops:
  0.6 0.0 copy-start
  0.6 3.2 %broadcast_in_dim.30 = f32[32,64,2,128]{3,2,1,0:T(2,128)} broadcast(f32[64,2,128]{2,1,0:T(2,128)} %param.10), dimensions={1,2,3} | broadcast | bytes 2162688 | tf_op jit(solution)/shard_map/broadcast_in_dim | solution.py:10
  3.8 8.6 %all-to-all-start = ((f32[32,64,2,128]{3,2,1,0:T(2,128)}), f32[32,64,2,128]{3,2,1,0:T(2,128)S(1)}, u32[]{:S(2)}, u32[]{:S(2)}) async-start(f32[32,64,2,128]{3,2,1,0:T(2,128)} %broadcast_in_dim.30), calls=%async_computation | async-start | bytes 4194304 | tf_op jit(solution)/shard_map/all_to_all | solution.py:9
  12.4 0.7 add_multiply_fusion
  13.1 0.8 copy.65
  13.9 0.1 copy.66
  14.0 0.2 copy.67
  14.2 0.4 add.85
  14.6 0.3 copy.69
  14.9 11.3 %bitcast_convert_fusion = f32[512,8,8,128]{3,2,1,0:T(8,128)} fusion(bf16[256,1,2,8,8,128]{5,4,3,2,1,0:T(8,128)(2,1)} %param.11), kind=kLoop, calls=%fused_computation.33 | loop fusion | flops 4194304 | bytes 25165824
  26.2 14.6 %all-to-all-done = f32[32,64,2,128]{3,2,1,0:T(2,128)S(1)} async-done(((f32[32,64,2,128]{3,2,1,0:T(2,128)}), f32[32,64,2,128]{3,2,1,0:T(2,128)S(1)}, u32[]{:S(2)}, u32[]{:S(2)}) %all-to-all-start) | async-done | bytes 2097184 | tf_op jit(solution)/shard_map/all_to_all | solution.py:9
  40.8 2.5 %copy.63 = f32[64,32,2,128]{3,2,1,0:T(2,128)} copy(f32[64,32,2,128]{3,2,0,1:T(2,128)S(1)} %bitcast.36) | data formatting | bytes 4194304 | tf_op jit(solution)/shard_map/transpose | solution.py:15
  43.3 2.9 %reshape_reshape.6 = f32[512,1024]{1,0:T(8,128)S(1)} reshape(f32[64,32,2,128]{3,2,1,0:T(2,128)} %copy.63) | data formatting | bytes 4194304 | tf_op jit(solution)/shard_map/reshape;reshape | solution.py:60
  46.2 18.6 %gather_fusion = f32[4096,1024]{1,0:T(8,128)} fusion(f32[512,1024]{1,0:T(8,128)S(1)} %reshape_reshape.6, s32[4096]{0:T(1024)S(1)} %broadcast_clamp_fusion), kind=kCustom, calls=%fused_computation | custom fusion | bytes 33570816 | tf_op jit(solution)/shard_map/jit(_take)/gather | solution.py:66
  64.8 0.0 copy-start.4
  64.8 0.0 copy-start.6
  64.9 0.0 copy-start.5
  64.9 13.5 %fusion.3 = f32[256,2]{1,0:T(8,128)S(1)} fusion(f32[256,1,2,8,8,128]{5,3,4,2,0,1:T(8,128)} %bitcast.34, pred[256,2,8]{2,1,0:T(4,128)(4,1)S(1)} %copy.69, bf16[256,1,2,8,8,128]{5,4,3,2,1,0:T(8,128)(2,1)} %param.11), kind=kLoop, calls=%fused_computation.7 | loop fusion | flops 16776704 | bytes 25171968 | tf_op jit(solution)/shard_map/reduce_sum | solution.py:70
  78.3 0.0 copy-start.1
  78.3 0.1 select_reduce_fusion
  78.5 0.6 broadcast_in_dim.34
  79.1 8.2 %all-to-all-start.1 = ((f32[8,1,256]{2,1,0:T(1,128)}), f32[8,1,256]{2,1,0:T(1,128)S(1)}, u32[]{:S(2)}, u32[]{:S(2)}) async-start(f32[8,1,256]{2,1,0:T(1,128)} %broadcast_in_dim.34), calls=%async_computation.1 | async-start | bytes 16384 | tf_op jit(solution)/shard_map/all_to_all | solution.py:9
  87.2 0.0 copy-done.4
  87.3 0.0 copy-done.6
  87.3 0.1 select_reduce_fusion.1
  87.3 0.4 reshape.153
  87.7 6.1 %all-to-all-done.1 = f32[8,1,256]{2,1,0:T(1,128)S(1)} async-done(((f32[8,1,256]{2,1,0:T(1,128)}), f32[8,1,256]{2,1,0:T(1,128)S(1)}, u32[]{:S(2)}, u32[]{:S(2)}) %all-to-all-start.1) | async-done | bytes 8224 | tf_op jit(solution)/shard_map/all_to_all | solution.py:9
  93.9 0.0 copy-done.5
  93.9 0.0 copy-start.3
  93.9 0.1 bitcast_select_fusion
  94.0 0.3 broadcast_in_dim.58
  94.3 0.4 mul.46
  94.7 0.0 copy-start.2
  94.7 43.7 %scatter_custom_fusion = f32[512,1024]{1,0:T(8,128)} fusion(s32[4096]{0:T(1024)S(1)} %reshape.153, f32[512,8,8,128]{3,2,1,0:T(8,128)} %bitcast_convert_fusion, f32[4096]{0:T(1024)S(1)} %mul.46, f32[]{:T(128)} %constant.30.clone.1), kind=kCustom, calls=%fused_computation.3 | custom fusion | flops 8388608 | bytes 18890756 | tf_op jit(solution)/shard_map/scatter-add | solution.py:79
  138.4 4.0 %reshape_reshape.7 = f32[64,32,2,128]{3,2,1,0:T(2,128)} reshape(f32[512,1024]{1,0:T(8,128)} %scatter_custom_fusion) | data formatting | bytes 4194304 | tf_op jit(solution)/shard_map/reshape;reshape | solution.py:31
  142.4 4.1 %copy.74 = f32[32,64,2,128]{3,2,1,0:T(2,128)} copy(f32[32,64,2,128]{3,2,0,1:T(2,128)} %bitcast.37) | data formatting | bytes 4194304 | tf_op jit(solution)/shard_map/transpose | solution.py:32
  146.5 6.6 %all-to-all-start.2 = ((f32[32,64,2,128]{3,2,1,0:T(2,128)}), f32[32,64,2,128]{3,2,1,0:T(2,128)}, u32[]{:S(2)}, u32[]{:S(2)}) async-start(f32[32,64,2,128]{3,2,1,0:T(2,128)} %copy.74), calls=%async_computation.2 | async-start | bytes 4194304 | tf_op jit(solution)/shard_map/all_to_all | solution.py:37
  153.1 0.0 copy-done.1
  153.1 1.8 convolution_bitcast_fusion
  154.9 0.0 copy-done.3
  154.9 14.7 %all_gather.3 = f32[64,2,1024]{2,1,0:T(2,128)S(1)} all-gather(f32[64,2,128]{2,1,0:T(2,128)S(1)} %convolution_bitcast_fusion), channel_id=1, replica_groups=mesh['rec'=32,'tile'=8] {'tile'}, dimensions={2}, use_global_device_ids=true | all-gather | bytes 589824 | tf_op jit(solution)/shard_map/all_gather | solution.py:85
  169.6 0.0 copy-done
  169.6 0.7 fusion.7
  170.3 11.3 %all-to-all-done.2 = f32[32,64,2,128]{3,2,1,0:T(2,128)} async-done(((f32[32,64,2,128]{3,2,1,0:T(2,128)}), f32[32,64,2,128]{3,2,1,0:T(2,128)}, u32[]{:S(2)}, u32[]{:S(2)}) %all-to-all-start.2) | async-done | bytes 2097184 | tf_op jit(solution)/shard_map/all_to_all | solution.py:37
  181.6 2.3 %reduce_sum.53 = f32[64,2,128]{2,1,0:T(2,128)S(1)} reduce(f32[32,64,2,128]{3,2,1,0:T(2,128)} %all-to-all-done.2, f32[]{:T(128)} %constant.30.clone.1), dimensions={0}, to_apply=%region_5.6 | reduce | flops 507904 | bytes 2162692 | tf_op jit(solution)/shard_map/reduce_sum | solution.py:38
  183.8 0.0 copy-done.2
  183.8 0.2 fusion.5
  184.0 0.7 copy.76
  (7 shorter events, 0.1 us)
Async XLA Ops:
  0.6 168.9 %copy-start = (f32[128,1024]{1,0:T(8,128)S(1)}, f32[128,1024]{1,0:T(8,128)}, u32[]{:S(2)}) copy-start(f32[128,1024]{1,0:T(8,128)} %param.19) | copy-start | bytes 1572868
  3.8 36.9 %all-to-all-start = ((f32[32,64,2,128]{3,2,1,0:T(2,128)}), f32[32,64,2,128]{3,2,1,0:T(2,128)S(1)}, u32[]{:S(2)}, u32[]{:S(2)}) async-start(f32[32,64,2,128]{3,2,1,0:T(2,128)} %broadcast_in_dim.30), calls=%async_computation | async-start | bytes 4194304 | tf_op jit(solution)/shard_map/all_to_all | solution.py:9
  64.8 22.4 %copy-start.4 = (s32[256]{0:T(256)S(1)}, s32[256]{0:T(256)}, u32[]{:S(2)}) copy-start(s32[256]{0:T(256)} %param.15) | copy-start | bytes 3076
  64.8 22.4 %copy-start.6 = (f32[4]{0:T(128)S(1)}, f32[4]{0:T(128)}, u32[]{:S(2)}) copy-start(f32[4]{0:T(128)} %param.16) | copy-start | bytes 52
  64.9 29.0 %copy-start.5 = (f32[256]{0:T(256)S(1)}, f32[256]{0:T(256)}, u32[]{:S(2)}) copy-start(f32[256]{0:T(256)} %param.14) | copy-start | bytes 3076
  78.3 74.8 %copy-start.1 = (f32[64,32,2,128]{3,2,1,0:T(2,128)S(1)}, f32[64,32,2,128]{3,2,1,0:T(2,128)}, u32[]{:S(2)}) copy-start(f32[64,32,2,128]{3,2,1,0:T(2,128)} %copy.63) | copy-start | bytes 6291460
  79.1 14.8 %all-to-all-start.1 = ((f32[8,1,256]{2,1,0:T(1,128)}), f32[8,1,256]{2,1,0:T(1,128)S(1)}, u32[]{:S(2)}, u32[]{:S(2)}) async-start(f32[8,1,256]{2,1,0:T(1,128)} %broadcast_in_dim.34), calls=%async_computation.1 | async-start | bytes 16384 | tf_op jit(solution)/shard_map/all_to_all | solution.py:9
  93.9 61.0 %copy-start.3 = (f32[256]{0:T(256)}, f32[256]{0:T(256)S(1)}, u32[]{:S(2)}) copy-start(f32[256]{0:T(256)S(1)} %subtract_divide_fusion) | copy-start | bytes 3076
  94.7 89.2 %copy-start.2 = (f32[64,64]{1,0:T(8,128)S(1)}, f32[64,64]{1,0:T(8,128)}, u32[]{:S(2)}) copy-start(f32[64,64]{1,0:T(8,128)} %param.17) | copy-start | bytes 49156
  146.5 35.1 %all-to-all-start.2 = ((f32[32,64,2,128]{3,2,1,0:T(2,128)}), f32[32,64,2,128]{3,2,1,0:T(2,128)}, u32[]{:S(2)}, u32[]{:S(2)}) async-start(f32[32,64,2,128]{3,2,1,0:T(2,128)} %copy.74), calls=%async_computation.2 | async-start | bytes 4194304 | tf_op jit(solution)/shard_map/all_to_all | solution.py:37
where the time goes:
time: 185 us
  other arithmetic  71.8 us (39%)
  local copies, waits for them, and re-layouts  39.4 us (21%)
  waiting for transfers between devices  32 us (17%)
  starting transfers between devices  23.4 us (13%)
  blocking collectives  14.7 us (8%)
  matrix products  2.69 us (1%)
    scatter-add x1, other arithmetic, shards(): jax.ops.segment_sum(contrib, row_index, num_segments=periods * tiles_y)  43.7 us
    all_to_all x2, waiting for transfers between devices, copy_for_each(): lax.all_to_all(jnp.broadcast_to(value[None], (length, *value.shape)), axi...  20.7 us
    gather x1, local copies, waits for them, and re-layouts, shards(): picked = jnp.take(flux_table, row_index, axis=0)  18.6 us
    all_to_all x2, starting transfers between devices, copy_for_each(): lax.all_to_all(jnp.broadcast_to(value[None], (length, *value.shape)), axi...  16.8 us
    all_gather x1, blocking collectives, shards(): lax.all_gather(lat_done, 'tile', axis=2, tiled=True)  14.7 us
    reduce_sum x2, other arithmetic, shards(): partial_pred = jnp.sum(jnp.sum(products, axis=2) * active, axis=1)  13.6 us
    all_to_all x1, waiting for transfers between devices, sent_and_summed(): lax.all_to_all(in_blocks(value, dim, length), axis, 0, 0, tiled=True)  11.3 us
    unnamed x1, other arithmetic  11.3 us
  transfers between devices with their start and end apart: 3, of which 3 were waited for; matrix products, arithmetic and copies ran while one was open for 9% of the time, Pallas kernels for 0%

commit v1 on v0

v1 whole, which is shorter than its diff:
```python
import functools

import jax
import jax.numpy as jnp
from jax import lax
from jax.experimental import pallas as pl
from jax.experimental.pallas import tpu as pltpu
from jax.sharding import PartitionSpec as P

MESH = pl.DeviceIdType.MESH
HIGHEST = lax.Precision.HIGHEST
F32 = jnp.float32
VMEM_LIMIT = 48 << 20

SIDE = 4
CORES = 2
PERIODS = 64
HALF = 32
WINDOW = 8
TILES = 8
ROWS = (TILES + 1) * PERIODS
RECEPTORS = 256
STRIPS = 8
CHUNKS = 8
PER_CHUNK = RECEPTORS // CHUNKS
GROUP = 8


def place():
    rec = lax.axis_index("rec")
    return rec // 8, (rec // 2) % SIDE, rec % 2, lax.axis_index("tile")


def rec_of(x, y, c):
    return ((x % SIDE) * SIDE + (y % SIDE)) * CORES + c


def tile_of(x, y):
    return 2 * (x % SIDE) + (y % SIDE) // 2


def pair_of(y, c):
    return pl.multiple_of(4 * ((y % SIDE) % 2) + 2 * c, 2)


def meet(peers):
    barrier = pltpu.get_barrier_semaphore()
    for peer in peers:
        pl.semaphore_signal(barrier, inc=1, device_id=peer, device_id_type=MESH)
    pl.semaphore_wait(barrier, len(peers))


def plane_peers(x, y, c, z):
    peers = [(rec_of(x, y, 1 - c), z)]
    peers += [(rec_of(x + d, y, c), z) for d in (1, 2, 3)]
    peers += [(rec_of(x, y + d, c), z) for d in (1, 2, 3)]
    return peers


def copy_to(src, dst, send, recv, peer):
    return pltpu.make_async_remote_copy(
        src_ref=src, dst_ref=dst, send_sem=send, recv_sem=recv, device_id=peer, device_id_type=MESH
    )


def forward_kernel(
    slots,
    starts,
    group_var,
    dev,
    dev_rows,
    foot,
    observed,
    group,
    inv_time,
    inv_lat,
    inv_lon,
    misfit_out,
    prior_out,
    lat_out,
    strip,
    blocks,
    sums,
    field,
    shares,
    own_share,
    send_sem,
    recv_sem,
    z_send,
    z_recv,
    s_send,
    s_recv,
    f_sem,
    l_sem,
):
    x, y, c, z = place()
    me = rec_of(x, y, c)
    partner = (rec_of(x, y, 1 - c), z)
    loads = []
    for n in range(CHUNKS):
        load = pltpu.make_async_copy(
            foot.at[pl.ds(n * PER_CHUNK, PER_CHUNK), 0], blocks.at[pl.ds(n * PER_CHUNK, PER_CHUNK)], f_sem.at[n]
        )
        load.start()
        loads.append(load)

    def spot(sx, sy, sc, first, count):
        return strip.at[
            pl.ds(pl.multiple_of(PERIODS * (1 + tile_of(sx, sy)) + first, HALF), count), pl.ds(pair_of(sy, sc), 2), :
        ]

    own_local = pltpu.make_async_copy(dev, spot(x, y, c, 0, PERIODS), l_sem.at[0])
    own_local.start()
    own_field = pltpu.make_async_copy(dev_rows, field.at[z], l_sem.at[1])
    own_field.start()
    meet(plane_peers(x, y, c, z) + [(me, (z + d) % STRIPS) for d in range(1, STRIPS)])

    count = [0]
    pending = []

    def send(src, where, peer):
        n = count[0]
        count[0] += 1
        one = copy_to(src, where, send_sem.at[n], recv_sem.at[n], peer)
        one.start()
        pending.append(one)
        return n

    def arrived(n, where):
        copy_to(where, where, send_sem.at[n], recv_sem.at[n], partner).wait_recv()

    first_a, first_b = dev.at[pl.ds(0, HALF)], dev.at[pl.ds(HALF, HALF)]
    in_a = [send(first_a, spot(x, y, c, 0, HALF), (rec_of(x + d, y, c), z)) for d in (1, 2, 3)]
    in_b = [send(first_b, spot(x, y, c, HALF, HALF), (rec_of(x, y + d, c), z)) for d in (1, 2, 3)]
    far_a = [[send(first_a, spot(x, y, c, 0, HALF), (rec_of(x, y + d, c), z)) for d in (1, 2, 3)]]
    far_b = [[send(first_b, spot(x, y, c, HALF, HALF), (rec_of(x + d, y, c), z)) for d in (1, 2, 3)]]
    near = send(dev, spot(x, y, c, 0, PERIODS), partner)
    from_partner = [(near, lambda: spot(x, y, 1 - c, 0, PERIODS))]
    z_copies = []
    for d in range(1, STRIPS):
        one = copy_to(dev_rows, field.at[z], z_send.at[d - 1], z_recv.at[d - 1], (me, (z + d) % STRIPS))
        one.start()
        z_copies.append(one)

    strip[pl.ds(0, PERIODS)] = jnp.zeros((PERIODS, 8, 128), F32)

    wide = (lax.broadcasted_iota(jnp.int32, (2 * PERIODS, PERIODS), 0) // 2
            == lax.broadcasted_iota(jnp.int32, (2 * PERIODS, PERIODS), 1)).astype(F32)
    time_rows = jnp.dot(wide, inv_time[...], precision=HIGHEST, preferred_element_type=F32)
    time_both = lax.dot_general(time_rows, wide, (((1,), (1,)), ((), ())), precision=HIGHEST, preferred_element_type=F32)
    square = (2 * PERIODS, 2 * PERIODS)
    same = lax.broadcasted_iota(jnp.int32, square, 0) % 2 == lax.broadcasted_iota(jnp.int32, square, 1) % 2
    time_both = jnp.where(same, time_both, 0.0)
    for n in range(2):
        pick = (lax.broadcasted_iota(jnp.int32, (64, 128), 0) == 2 * me + n).astype(F32)
        lat_out[n] = jnp.dot(inv_lat[...], pick, precision=HIGHEST, preferred_element_type=F32)

    for d in (1, 2, 3):
        arrived(in_a[d - 1], spot(x - d, y, c, 0, HALF))
        here = spot(x - d, y, c, 0, HALF)
        far_a.append([send(here, here, (rec_of(x, y + e, c), z)) for e in (1, 2, 3)])
        n = send(here, here, partner)
        from_partner.append((n, functools.partial(spot, x - d, y, 1 - c, 0, HALF)))
        arrived(in_b[d - 1], spot(x, y - d, c, HALF, HALF))
        here = spot(x, y - d, c, HALF, HALF)
        far_b.append([send(here, here, (rec_of(x + e, y, c), z)) for e in (1, 2, 3)])
        n = send(here, here, partner)
        from_partner.append((n, functools.partial(spot, x, y - d, 1 - c, HALF, HALF)))
    for d in range(4):
        for e in (1, 2, 3):
            here = spot(x - d, y - e, c, 0, HALF)
            arrived(far_a[d][e - 1], here)
            n = send(here, here, partner)
            from_partner.append((n, functools.partial(spot, x - d, y - e, 1 - c, 0, HALF)))
            here = spot(x - e, y - d, c, HALF, HALF)
            arrived(far_b[d][e - 1], here)
            n = send(here, here, partner)
            from_partner.append((n, functools.partial(spot, x - e, y - d, 1 - c, HALF, HALF)))
    for n, where in from_partner:
        arrived(n, where())
    own_local.wait()
    for load in loads:
        load.wait()

    def group_sums(i, carry):
        totals = []
        for u in range(GROUP):
            r = i * GROUP + u
            start = starts[r]
            parts = []
            for k in range(2):
                base = (slots[k, r] + 1) * PERIODS + start
                parts.append(strip[pl.ds(base, WINDOW)] * blocks[r, k].astype(F32))
            totals.append(jnp.sum(parts[0] + parts[1], axis=0))
        sums[pl.ds(pl.multiple_of(i * GROUP, GROUP), GROUP), :] = jnp.sum(jnp.stack(totals), axis=1)
        return carry

    lax.fori_loop(0, RECEPTORS // GROUP, group_sums, 0)
    share = lax.dot_general(
        jnp.ones((8, 128), F32), sums[...], (((1,), (1,)), ((), ())), precision=HIGHEST, preferred_element_type=F32
    )
    own_share[...] = share
    s_copies = []
    for d in range(1, STRIPS):
        one = copy_to(
            own_share.at[pl.ds(0, 1), :], shares.at[pl.ds(z, 1), :], s_send.at[d - 1], s_recv.at[d - 1],
            (me, (z + d) % STRIPS),
        )
        one.start()
        s_copies.append(one)
    mine = pltpu.make_async_copy(own_share.at[pl.ds(0, 1), :], shares.at[pl.ds(z, 1), :], l_sem.at[2])
    mine.start()

    own_field.wait()
    for one in z_copies:
        one.wait()
    lon_done = jnp.zeros((2 * PERIODS, 128), F32)
    for s in range(STRIPS):
        lon_done += lax.dot_general(
            field[s], inv_lon[:, s * 128 : (s + 1) * 128], (((1,), (1,)), ((), ())),
            precision=HIGHEST, preferred_element_type=F32,
        )
    prior_out[...] = jnp.dot(time_both, lon_done, precision=HIGHEST, preferred_element_type=F32)

    mine.wait()
    for one in s_copies:
        one.wait()
    predicted = jnp.sum(shares[...], axis=0, keepdims=True)
    variance = jnp.zeros((1, RECEPTORS), F32)
    for g in range(4):
        variance += jnp.where(group[...] == g, group_var[g], 0.0)
    misfit_out[...] = (predicted - observed[...]) / variance
    for one in pending:
        one.wait_send()


def adjoint_kernel(slots, starts, misfit, foot, prior, lat, misfit_row, total, misfit_out, blocks, second, f_sem):
    loads = []
    for n in range(CHUNKS):
        load = pltpu.make_async_copy(
            foot.at[pl.ds(n * PER_CHUNK, PER_CHUNK), 0], blocks.at[pl.ds(n * PER_CHUNK, PER_CHUNK)], f_sem.at[n]
        )
        load.start()
        loads.append(load)
    misfit_out[...] = misfit_row[...]
    second[...] = jnp.zeros((ROWS, 8, 128), F32)
    total[pl.ds(0, PERIODS)] = jnp.zeros((PERIODS, 8, 128), F32)

    def one_period(p, carry):
        first = jnp.broadcast_to(prior[pl.ds(2 * p, 1), :], (8, 128))
        other = jnp.broadcast_to(prior[pl.ds(2 * p + 1, 1), :], (8, 128))
        for t in range(TILES):
            rows = slice(8 * t, 8 * t + 8)
            total[PERIODS * (1 + t) + p] = lat[0, rows, :] * first + lat[1, rows, :] * other
        return carry

    lax.fori_loop(0, PERIODS, one_period, 0)

    def pair(i, carry):
        held = []
        for u, into in ((0, total), (1, second)):
            r = 2 * i + u
            start = starts[r]
            weight = misfit[r]
            for k in range(2):
                rows = pl.ds((slots[k, r] + 1) * PERIODS + start, WINDOW)
                held.append((into, rows, into[rows] + blocks[r, k].astype(F32) * weight))
        for into, rows, value in held:
            into[rows] = value
        return carry

    for n in range(CHUNKS):
        loads[n].wait()
        lax.fori_loop(n * PER_CHUNK // 2, (n + 1) * PER_CHUNK // 2, pair, 0)

    def join(i, carry):
        rows = pl.ds(pl.multiple_of(PERIODS + i * 16, 16), 16)
        total[rows] = total[rows] + second[rows]
        return carry

    lax.fori_loop(0, TILES * PERIODS // 16, join, 0)


def scatter_kernel(
    part, out, got, both, a_got, a_sum, a_last, b_got, b_sum, b_last, done, e_send, e_recv, send_sem, recv_sem, l_sem
):
    x, y, c, z = place()
    partner = (rec_of(x, y, 1 - c), z)
    meet(plane_peers(x, y, c, z))
    swaps = []
    for half in range(2):
        for h in range(2):
            n = 2 * half + h
            theirs = pl.ds(pl.multiple_of(4 * h + 2 * (1 - c), 2), 2)
            periods = pl.ds(half * HALF, HALF)
            one = copy_to(
                part.at[pl.ds(1, TILES), periods, theirs, :], got.at[:, periods, theirs, :],
                e_send.at[n], e_recv.at[n], partner,
            )
            one.start()
            swaps.append(one)
    my_tile = tile_of(x, y)
    my_th = y // 2
    my_pair = pl.ds(pair_of(y, c), 2)
    pending = []

    def send(n, src, dst, peer):
        one = copy_to(src, dst, send_sem.at[n], recv_sem.at[n], peer)
        one.start()
        pending.append(one)
        return one

    def add_half(half):
        def step(t, carry):
            periods = pl.ds(half * HALF, HALF)
            both[t, periods] = part[1 + t, periods] + got[t, periods]
            return carry

        lax.fori_loop(0, TILES, step, 0)

    swaps[0].wait_recv()
    swaps[1].wait_recv()
    add_half(0)
    a_copies = []
    for d in (1, 2, 3):
        for h in range(2):
            rows = pl.ds(pl.multiple_of(4 * h + 2 * c, 2), 2)
            a_copies.append(send(
                2 * (d - 1) + h,
                both.at[pl.ds(2 * ((x + d) % SIDE), 2), pl.ds(0, HALF), rows, :],
                a_got.at[d - 1, :, :, rows, :],
                (rec_of(x + d, y, c), z),
            ))
    swaps[2].wait_recv()
    swaps[3].wait_recv()
    add_half(1)
    b_copies = []
    for d in (1, 2, 3):
        rows = pl.ds(pair_of(y + d, c), 2)
        for s in range(SIDE):
            b_copies.append(send(
                6 + 4 * (d - 1) + s,
                both.at[2 * s + ((y + d) % SIDE) // 2, pl.ds(HALF, HALF), rows, :],
                b_got.at[d - 1, s, :, rows, :],
                (rec_of(x, y + d, c), z),
            ))
    for one in a_copies:
        one.wait_recv()
    for th in range(2):
        a_sum[th] = both[2 * x + th, pl.ds(0, HALF)] + a_got[0, th] + a_got[1, th] + a_got[2, th]
    a_final = []
    for d in (1, 2, 3):
        rows = pl.ds(pair_of(y + d, c), 2)
        a_final.append(send(
            18 + d - 1, a_sum.at[((y + d) % SIDE) // 2, :, rows, :], a_last.at[d - 1, :, rows, :],
            (rec_of(x, y + d, c), z),
        ))
    for one in b_copies:
        one.wait_recv()
    for s in range(SIDE):
        b_sum[s] = both[2 * s + my_th, pl.ds(HALF, HALF)] + b_got[0, s] + b_got[1, s] + b_got[2, s]
    b_final = []
    for d in (1, 2, 3):
        b_final.append(send(
            21 + d - 1, b_sum.at[(x + d) % SIDE, :, my_pair, :], b_last.at[d - 1, :, my_pair, :],
            (rec_of(x + d, y, c), z),
        ))
    for one in a_final:
        one.wait_recv()
    done[pl.ds(0, HALF)] = a_sum[my_th] + a_last[0] + a_last[1] + a_last[2]
    for one in b_final:
        one.wait_recv()
    done[pl.ds(HALF, HALF)] = b_sum[x] + b_last[0] + b_last[1] + b_last[2]
    final = pltpu.make_async_copy(done.at[:, my_pair, :], out, l_sem)
    final.start()
    for one in swaps + pending:
        one.wait_send()
    final.wait()


def shards(
    deviation, footprint, tile_list, offset, observed, obs_group, group_var, inv_time, inv_lat, inv_lon
):
    vmem = pl.BlockSpec(memory_space=pltpu.VMEM)
    smem = pl.BlockSpec(memory_space=pltpu.SMEM)
    hbm = pl.BlockSpec(memory_space=pl.ANY)
    slots = jnp.transpose(tile_list, (1, 2, 0)).reshape(2, RECEPTORS)
    copies = 61
    misfit_row, prior, lat = pl.pallas_call(
        forward_kernel,
        name="forward",
        out_shape=(
            jax.ShapeDtypeStruct((1, RECEPTORS), F32),
            jax.ShapeDtypeStruct((2 * PERIODS, 128), F32),
            jax.ShapeDtypeStruct((2, 64, 128), F32),
        ),
        in_specs=[smem, smem, smem, vmem, vmem, hbm, vmem, vmem, vmem, vmem, vmem],
        out_specs=(vmem, vmem, vmem),
        scratch_shapes=[
            pltpu.VMEM((ROWS, 8, 128), F32),
            pltpu.VMEM((RECEPTORS, 2, WINDOW, 8, 128), jnp.bfloat16),
            pltpu.VMEM((RECEPTORS, 128), F32),
            pltpu.VMEM((STRIPS, 2 * PERIODS, 128), F32),
            pltpu.VMEM((STRIPS, RECEPTORS), F32),
            pltpu.VMEM((8, RECEPTORS), F32),
            pltpu.SemaphoreType.DMA((copies,)),
            pltpu.SemaphoreType.DMA((copies,)),
            pltpu.SemaphoreType.DMA((7,)),
            pltpu.SemaphoreType.DMA((7,)),
            pltpu.SemaphoreType.DMA((7,)),
            pltpu.SemaphoreType.DMA((7,)),
            pltpu.SemaphoreType.DMA((CHUNKS,)),
            pltpu.SemaphoreType.DMA((3,)),
        ],
        compiler_params=pltpu.CompilerParams(collective_id=0, has_side_effects=True, vmem_limit_bytes=VMEM_LIMIT),
    )(
        slots,
        offset,
        group_var,
        deviation,
        deviation.reshape(2 * PERIODS, 128),
        footprint,
        observed.reshape(1, RECEPTORS),
        obs_group.reshape(1, RECEPTORS),
        inv_time,
        inv_lat,
        inv_lon,
    )
    total, misfit = pl.pallas_call(
        adjoint_kernel,
        name="adjoint",
        out_shape=(jax.ShapeDtypeStruct((ROWS, 8, 128), F32), jax.ShapeDtypeStruct((1, RECEPTORS), F32)),
        in_specs=[smem, smem, smem, hbm, vmem, vmem, vmem],
        out_specs=(vmem, vmem),
        scratch_shapes=[
            pltpu.VMEM((RECEPTORS, 2, WINDOW, 8, 128), jnp.bfloat16),
            pltpu.VMEM((ROWS, 8, 128), F32),
            pltpu.SemaphoreType.DMA((CHUNKS,)),
        ],
        compiler_params=pltpu.CompilerParams(vmem_limit_bytes=VMEM_LIMIT),
    )(slots, offset, misfit_row.reshape(RECEPTORS), footprint, prior, lat, misfit_row)
    gradient = pl.pallas_call(
        scatter_kernel,
        name="scatter",
        out_shape=jax.ShapeDtypeStruct((PERIODS, 2, 128), F32),
        in_specs=[vmem],
        out_specs=hbm,
        scratch_shapes=[
            pltpu.VMEM((TILES, PERIODS, 8, 128), F32),
            pltpu.VMEM((TILES, PERIODS, 8, 128), F32),
            pltpu.VMEM((3, 2, HALF, 8, 128), F32),
            pltpu.VMEM((2, HALF, 8, 128), F32),
            pltpu.VMEM((3, HALF, 8, 128), F32),
            pltpu.VMEM((3, SIDE, HALF, 8, 128), F32),
            pltpu.VMEM((SIDE, HALF, 8, 128), F32),
            pltpu.VMEM((3, HALF, 8, 128), F32),
            pltpu.VMEM((PERIODS, 8, 128), F32),
            pltpu.SemaphoreType.DMA((4,)),
            pltpu.SemaphoreType.DMA((4,)),
            pltpu.SemaphoreType.DMA((24,)),
            pltpu.SemaphoreType.DMA((24,)),
            pltpu.SemaphoreType.DMA,
        ],
        compiler_params=pltpu.CompilerParams(collective_id=1, has_side_effects=True, vmem_limit_bytes=VMEM_LIMIT),
    )(total.reshape(TILES + 1, PERIODS, 8, 128))
    return gradient, misfit.reshape(RECEPTORS)


def solution(mesh):
    return jax.shard_map(
        shards,
        mesh=mesh,
        in_specs=(
            P(None, "rec", "tile"),
            P("rec", "tile", None, None, None, None),
            P("rec", "tile", None),
            P("rec"),
            P("rec"),
            P("rec"),
            P(),
            P(),
            P(),
            P("tile", None),
        ),
        out_specs=(P(None, "rec", "tile"), P("rec")),
        check_vma=False,
    )
```

time: 185 us -> 59.3 us (0.32)
  other arithmetic: 71.8 us -> 0 us
  Pallas kernels: 0 us -> 50.9 us
  local copies, waits for them, and re-layouts: 39.4 us -> 7.39 us
  waiting for transfers between devices: 32 us -> 0 us
  starting transfers between devices: 23.4 us -> 0 us
  blocking collectives: 14.7 us -> 0 us
  matrix products: 2.69 us -> 0 us
    pallas_call x0 -> x3, Pallas kernels: none -> 50.9 us  [the longest x1 29.2 us: shards(): pl.pallas_call(forward_kernel, name='forward', out_shape=(jax.ShapeDtypeS...]
    scatter-add x1 -> x0, other arithmetic: 43.7 us -> none  [shards(): jax.ops.segment_sum(contrib, row_index, num_segments=periods * tiles_y)]
    all_to_all x3 -> x0, waiting for transfers between devices: 32 us -> none  [the longest x2 20.7 us: copy_for_each(): lax.all_to_all(jnp.broadcast_to(value[None], (length, *value.shape)), axi...]
    all_to_all x3 -> x0, starting transfers between devices: 23.4 us -> none  [the longest x2 16.8 us: copy_for_each(): lax.all_to_all(jnp.broadcast_to(value[None], (length, *value.shape)), axi...]
    gather x1 -> x0, local copies, waits for them, and re-layouts: 18.6 us -> none  [shards(): picked = jnp.take(flux_table, row_index, axis=0)]
    reduce_sum x5 -> x0, other arithmetic: 16 us -> none  [the longest x2 13.6 us: shards(): partial_pred = jnp.sum(jnp.sum(products, axis=2) * active, axis=1)]
    all_gather x1 -> x0, blocking collectives: 14.7 us -> none  [shards(): lax.all_gather(lat_done, 'tile', axis=2, tiled=True)]
    unnamed x1 -> x0, other arithmetic: 11.3 us -> none
  transfers between devices with their start and end apart: 3 -> 0, of which waited for: 3 -> 0; matrix products, arithmetic and copies ran while one was open for 9% -> 0% of each run, Pallas kernels for 0% -> 0%
where the time goes in v1:
time: 59.3 us; the launch traced here: 58.9 us
  Pallas kernels  50.9 us (86%)
  local copies, waits for them, and re-layouts  7.39 us (12%)
  between operations  0.67 us (1%)
    pallas_call x1, Pallas kernels, shards(): pl.pallas_call(forward_kernel, name='forward', out_shape=(jax.ShapeDtypeS...  29.2 us
    pallas_call x1, Pallas kernels, shards(): pl.pallas_call(scatter_kernel, name='scatter', out_shape=jax.ShapeDtypeSt...  16.3 us
    unnamed x19, local copies, waits for them, and re-layouts  7.39 us
    pallas_call x1, Pallas kernels, shards(): pl.pallas_call(adjoint_kernel, name='adjoint', out_shape=(jax.ShapeDtypeS...  5.37 us

profile of v1, /device:TPU:1, one launch (start us, length us, event | category | flops | bytes accessed | tf_op | source)
XLA Modules:
  0.0 58.9 jit_solution(17870948207256220487)
XLA Ops:
  0.6 0.0 copy-start
  0.6 1.0 %copy-done = f32[128,1024]{1,0:T(8,128)S(1)} copy-done((f32[128,1024]{1,0:T(8,128)S(1)}, f32[128,1024]{1,0:T(8,128)}, u32[]{:S(2)}) %copy-start) | copy-done | bytes 524312
  1.7 0.0 copy-start.1
  1.7 0.8 %copy-done.1 = f32[64,2,128]{2,1,0:T(2,128)S(1)} copy-done((f32[64,2,128]{2,1,0:T(2,128)S(1)}, f32[64,2,128]{2,1,0:T(2,128)}, u32[]{:S(2)}) %copy-start.1) | copy-done | bytes 65560
  2.5 0.0 copy-start.2
  2.5 0.8 %copy-done.2 = f32[64,64]{1,0:T(8,128)S(1)} copy-done((f32[64,64]{1,0:T(8,128)S(1)}, f32[64,64]{1,0:T(8,128)}, u32[]{:S(2)}) %copy-start.2) | copy-done | bytes 16408
  3.3 0.0 copy-start.3
  3.3 0.8 %copy-done.3 = f32[64,64]{1,0:T(8,128)S(1)} copy-done((f32[64,64]{1,0:T(8,128)S(1)}, f32[64,64]{1,0:T(8,128)}, u32[]{:S(2)}) %copy-start.3) | copy-done | bytes 16408
  4.0 0.0 copy-start.4
  4.0 0.7 %copy-done.4 = s32[256,1,2]{0,2,1:T(2,128)S(1)} copy-done((s32[256,1,2]{0,2,1:T(2,128)S(1)}, s32[256,1,2]{0,2,1:T(2,128)}, u32[]{:S(2)}) %copy-start.4) | copy-done | bytes 2072
  4.7 0.0 copy-start.5
  4.7 0.7 %copy-done.5 = s32[256]{0:T(256)S(1)} copy-done((s32[256]{0:T(256)S(1)}, s32[256]{0:T(256)}, u32[]{:S(2)}) %copy-start.5) | copy-done | bytes 1048
  5.4 0.0 copy-start.6
  5.4 0.7 %copy-done.6 = f32[256]{0:T(256)S(1)} copy-done((f32[256]{0:T(256)S(1)}, f32[256]{0:T(256)}, u32[]{:S(2)}) %copy-start.6) | copy-done | bytes 1048
  6.1 0.0 copy-start.7
  6.1 0.7 %copy-done.7 = s32[256]{0:T(256)S(1)} copy-done((s32[256]{0:T(256)S(1)}, s32[256]{0:T(256)}, u32[]{:S(2)}) %copy-start.7) | copy-done | bytes 1048
  6.8 0.0 copy-start.8
  6.8 0.7 %copy-done.8 = f32[4]{0:T(128)S(1)} copy-done((f32[4]{0:T(128)S(1)}, f32[4]{0:T(128)}, u32[]{:S(2)}) %copy-start.8) | copy-done | bytes 40
  7.4 29.2 %forward.1 = (f32[1,256]{1,0:T(1,128)S(1)}, f32[128,128]{1,0:T(8,128)S(1)}, f32[2,64,128]{2,1,0:T(8,128)S(1)}) custom-call(s32[2,256]{1,0:T(2,128)S(1)} %bitcast.11, s32[256]{0:T(256)S(1)} %copy-done.5, f32[4]{0:T(128)S(1)} %copy-done.8, f32[64,2,128]{2,1,0:T(2,128)S(1)} %copy-done.1, f32[128,128]{1,0:T(8,128)S(1)} %bitcast.10, ...), custom_call_target="tpu_custom_call" | custom-call | tf_op jit(solution)/shard_map/forward/pallas_call | solution.py:389
  36.6 5.4 %adjoint.1 = (f32[576,8,128]{2,1,0:T(8,128)S(1)}, f32[1,256]{1,0:T(1,128)}) custom-call(s32[2,256]{1,0:T(2,128)S(1)} %bitcast.12, s32[256]{0:T(256)S(1)} %copy-done.5, f32[256]{0:T(256)S(1)} %bitcast.13, bf16[256,1,2,8,8,128]{5,4,3,2,1,0:T(8,128)(2,1)} %foot.3, f32[128,128]{1,0:T(8,128)S(1)} %get-tuple-element.8.prior, ...), custom_call_target="tpu_custom_call" | custom-call | tf_op jit(solution)/shard_map/adjoint/pallas_call | solution.py:429
  42.0 16.3 %scatter.1 = f32[64,2,128]{2,1,0:T(2,128)S(1)} custom-call(f32[9,64,8,128]{3,2,1,0:T(8,128)S(1)} %bitcast.9), custom_call_target="tpu_custom_call" | custom-call | tf_op jit(solution)/shard_map/scatter/pallas_call | solution.py:442
  58.3 0.6 %copy.13 = f32[64,2,128]{2,1,0:T(2,128)} copy(f32[64,2,128]{2,1,0:T(2,128)S(1)} %scatter.1) | data formatting | bytes 131072
Async XLA Ops:
  0.6 1.0 %copy-start = (f32[128,1024]{1,0:T(8,128)S(1)}, f32[128,1024]{1,0:T(8,128)}, u32[]{:S(2)}) copy-start(f32[128,1024]{1,0:T(8,128)} %inv_lon.1) | copy-start | bytes 1572868
  1.7 0.8 %copy-start.1 = (f32[64,2,128]{2,1,0:T(2,128)S(1)}, f32[64,2,128]{2,1,0:T(2,128)}, u32[]{:S(2)}) copy-start(f32[64,2,128]{2,1,0:T(2,128)} %dev.1) | copy-start | bytes 196612
  2.5 0.8 %copy-start.2 = (f32[64,64]{1,0:T(8,128)S(1)}, f32[64,64]{1,0:T(8,128)}, u32[]{:S(2)}) copy-start(f32[64,64]{1,0:T(8,128)} %inv_time.1) | copy-start | bytes 49156
  3.3 0.8 %copy-start.3 = (f32[64,64]{1,0:T(8,128)S(1)}, f32[64,64]{1,0:T(8,128)}, u32[]{:S(2)}) copy-start(f32[64,64]{1,0:T(8,128)} %inv_lat.1) | copy-start | bytes 49156
  4.0 0.7 %copy-start.4 = (s32[256,1,2]{0,2,1:T(2,128)S(1)}, s32[256,1,2]{0,2,1:T(2,128)}, u32[]{:S(2)}) copy-start(s32[256,1,2]{0,2,1:T(2,128)} %param.12) | copy-start | bytes 6148
  4.7 0.7 %copy-start.5 = (s32[256]{0:T(256)S(1)}, s32[256]{0:T(256)}, u32[]{:S(2)}) copy-start(s32[256]{0:T(256)} %starts.3) | copy-start | bytes 3076
  5.4 0.7 %copy-start.6 = (f32[256]{0:T(256)S(1)}, f32[256]{0:T(256)}, u32[]{:S(2)}) copy-start(f32[256]{0:T(256)} %param.14) | copy-start | bytes 3076
  6.1 0.7 %copy-start.7 = (s32[256]{0:T(256)S(1)}, s32[256]{0:T(256)}, u32[]{:S(2)}) copy-start(s32[256]{0:T(256)} %param.15) | copy-start | bytes 3076
  6.8 0.7 %copy-start.8 = (f32[4]{0:T(128)S(1)}, f32[4]{0:T(128)}, u32[]{:S(2)}) copy-start(f32[4]{0:T(128)} %group_var.1) | copy-start | bytes 52

commit v2 on v1

--- a/solution.py
+++ b/solution.py
@@ -10,7 +10,7 @@
 MESH = pl.DeviceIdType.MESH
 HIGHEST = lax.Precision.HIGHEST
 F32 = jnp.float32
-VMEM_LIMIT = 48 << 20
+VMEM_LIMIT = 28 << 20
 
 SIDE = 4
 CORES = 2
@@ -19,6 +19,7 @@
 WINDOW = 8
 TILES = 8
 ROWS = (TILES + 1) * PERIODS
+SUM_ROWS = (TILES + 2) * PERIODS
 RECEPTORS = 256
 STRIPS = 8
 CHUNKS = 8
@@ -43,6 +44,10 @@
     return pl.multiple_of(4 * ((y % SIDE) % 2) + 2 * c, 2)
 
 
+def in_hbm(value):
+    return pltpu.with_memory_space_constraint(value, pltpu.HBM)
+
+
 def meet(peers):
     barrier = pltpu.get_barrier_semaphore()
     for peer in peers:
@@ -64,22 +69,31 @@
 
 
 def forward_kernel(
+    slots_hbm,
+    starts_hbm,
+    group_var_hbm,
+    dev,
+    dev_rows,
+    foot,
+    observed_hbm,
+    group_hbm,
+    inv_time_hbm,
+    inv_lat_hbm,
+    inv_lon_hbm,
+    misfit_out,
+    prior_out,
+    lat_out,
+    blocks,
     slots,
     starts,
     group_var,
-    dev,
-    dev_rows,
-    foot,
     observed,
     group,
     inv_time,
     inv_lat,
     inv_lon,
-    misfit_out,
-    prior_out,
-    lat_out,
+    i_sem,
     strip,
-    blocks,
     sums,
     field,
     shares,
@@ -96,13 +110,14 @@
     x, y, c, z = place()
     me = rec_of(x, y, c)
     partner = (rec_of(x, y, 1 - c), z)
-    loads = []
-    for n in range(CHUNKS):
-        load = pltpu.make_async_copy(
-            foot.at[pl.ds(n * PER_CHUNK, PER_CHUNK), 0], blocks.at[pl.ds(n * PER_CHUNK, PER_CHUNK)], f_sem.at[n]
-        )
+    small = []
+    for n, (src, dst) in enumerate((
+        (inv_time_hbm, inv_time), (inv_lat_hbm, inv_lat), (slots_hbm, slots), (starts_hbm, starts),
+        (group_var_hbm, group_var), (observed_hbm, observed), (group_hbm, group), (inv_lon_hbm, inv_lon),
+    )):
+        load = pltpu.make_async_copy(src, dst, i_sem.at[n])
         load.start()
-        loads.append(load)
+        small.append(load)
 
     def spot(sx, sy, sc, first, count):
         return strip.at[
@@ -142,7 +157,16 @@
         one.start()
         z_copies.append(one)
 
+    loads = []
+    for n in range(CHUNKS):
+        load = pltpu.make_async_copy(
+            foot.at[pl.ds(n * PER_CHUNK, PER_CHUNK), 0], blocks.at[pl.ds(n * PER_CHUNK, PER_CHUNK)], f_sem.at[n]
+        )
+        load.start()
+        loads.append(load)
     strip[pl.ds(0, PERIODS)] = jnp.zeros((PERIODS, 8, 128), F32)
+    for load in small:
+        load.wait()
 
     wide = (lax.broadcasted_iota(jnp.int32, (2 * PERIODS, PERIODS), 0) // 2
             == lax.broadcasted_iota(jnp.int32, (2 * PERIODS, PERIODS), 1)).astype(F32)
@@ -234,27 +258,25 @@
         one.wait_send()
 
 
-def adjoint_kernel(slots, starts, misfit, foot, prior, lat, misfit_row, total, misfit_out, blocks, second, f_sem):
-    loads = []
-    for n in range(CHUNKS):
-        load = pltpu.make_async_copy(
-            foot.at[pl.ds(n * PER_CHUNK, PER_CHUNK), 0], blocks.at[pl.ds(n * PER_CHUNK, PER_CHUNK)], f_sem.at[n]
-        )
+def adjoint_kernel(
+    slots_hbm, starts_hbm, misfit_hbm, blocks, misfit_row, total, second, misfit_out, slots, starts, misfit, i_sem
+):
+    small = []
+    for n, (src, dst) in enumerate(((slots_hbm, slots), (starts_hbm, starts), (misfit_hbm, misfit))):
+        load = pltpu.make_async_copy(src, dst, i_sem.at[n])
         load.start()
-        loads.append(load)
+        small.append(load)
     misfit_out[...] = misfit_row[...]
-    second[...] = jnp.zeros((ROWS, 8, 128), F32)
-    total[pl.ds(0, PERIODS)] = jnp.zeros((PERIODS, 8, 128), F32)
-
-    def one_period(p, carry):
-        first = jnp.broadcast_to(prior[pl.ds(2 * p, 1), :], (8, 128))
-        other = jnp.broadcast_to(prior[pl.ds(2 * p + 1, 1), :], (8, 128))
-        for t in range(TILES):
-            rows = slice(8 * t, 8 * t + 8)
-            total[PERIODS * (1 + t) + p] = lat[0, rows, :] * first + lat[1, rows, :] * other
+
+    def clear(i, carry):
+        rows = pl.ds(pl.multiple_of(i * 16, 16), 16)
+        total[rows] = jnp.zeros((16, 8, 128), F32)
+        second[rows] = jnp.zeros((16, 8, 128), F32)
         return carry
 
-    lax.fori_loop(0, PERIODS, one_period, 0)
+    lax.fori_loop(0, SUM_ROWS // 16, clear, 0)
+    for load in small:
+        load.wait()
 
     def pair(i, carry):
         held = []
@@ -263,117 +285,126 @@
             start = starts[r]
             weight = misfit[r]
             for k in range(2):
-                rows = pl.ds((slots[k, r] + 1) * PERIODS + start, WINDOW)
+                rows = pl.ds((slots[k, r] + 2) * PERIODS + start, WINDOW)
                 held.append((into, rows, into[rows] + blocks[r, k].astype(F32) * weight))
         for into, rows, value in held:
             into[rows] = value
         return carry
 
-    for n in range(CHUNKS):
-        loads[n].wait()
-        lax.fori_loop(n * PER_CHUNK // 2, (n + 1) * PER_CHUNK // 2, pair, 0)
-
-    def join(i, carry):
-        rows = pl.ds(pl.multiple_of(PERIODS + i * 16, 16), 16)
-        total[rows] = total[rows] + second[rows]
-        return carry
-
-    lax.fori_loop(0, TILES * PERIODS // 16, join, 0)
+    lax.fori_loop(0, RECEPTORS // 2, pair, 0)
+
+
+ORDER = (2, 1, 3, 0)
 
 
 def scatter_kernel(
-    part, out, got, both, a_got, a_sum, a_last, b_got, b_sum, b_last, done, e_send, e_recv, send_sem, recv_sem, l_sem
+    total, second, prior, lat, out, part, a_swap, a_both, a_got, a_sum, a_last, b_swap, b_both, b_got, b_sum, b_last,
+    done, send_sem, recv_sem, l_sem,
 ):
     x, y, c, z = place()
     partner = (rec_of(x, y, 1 - c), z)
-    meet(plane_peers(x, y, c, z))
-    swaps = []
-    for half in range(2):
-        for h in range(2):
-            n = 2 * half + h
-            theirs = pl.ds(pl.multiple_of(4 * h + 2 * (1 - c), 2), 2)
-            periods = pl.ds(half * HALF, HALF)
-            one = copy_to(
-                part.at[pl.ds(1, TILES), periods, theirs, :], got.at[:, periods, theirs, :],
-                e_send.at[n], e_recv.at[n], partner,
+    barrier = pltpu.get_barrier_semaphore()
+    peers = plane_peers(x, y, c, z)
+    for peer in peers:
+        pl.semaphore_signal(barrier, inc=1, device_id=peer, device_id_type=MESH)
+
+    def one_period(p, carry):
+        first = jnp.broadcast_to(prior[pl.ds(2 * p, 1), :], (8, 128))
+        other = jnp.broadcast_to(prior[pl.ds(2 * p + 1, 1), :], (8, 128))
+        for t in range(TILES):
+            rows = slice(8 * t, 8 * t + 8)
+            part[t // 2, t % 2, p] = (
+                total[1 + t // 2, t % 2, p] + second[1 + t // 2, t % 2, p]
+                + (lat[0, rows, :] * first + lat[1, rows, :] * other)
             )
-            one.start()
-            swaps.append(one)
-    my_tile = tile_of(x, y)
-    my_th = y // 2
-    my_pair = pl.ds(pair_of(y, c), 2)
+        return carry
+
+    lax.fori_loop(0, PERIODS, one_period, 0)
+    pl.semaphore_wait(barrier, len(peers))
+
+    first_half, second_half = pl.ds(0, HALF), pl.ds(HALF, HALF)
+    count = [0]
     pending = []
 
-    def send(n, src, dst, peer):
+    def send(src, dst, peer):
+        n = count[0]
+        count[0] += 1
         one = copy_to(src, dst, send_sem.at[n], recv_sem.at[n], peer)
         one.start()
         pending.append(one)
         return one
 
-    def add_half(half):
-        def step(t, carry):
-            periods = pl.ds(half * HALF, HALF)
-            both[t, periods] = part[1 + t, periods] + got[t, periods]
-            return carry
-
-        lax.fori_loop(0, TILES, step, 0)
-
-    swaps[0].wait_recv()
-    swaps[1].wait_recv()
-    add_half(0)
-    a_copies = []
-    for d in (1, 2, 3):
+    def pair_rows(sy, sc):
+        return pl.ds(pair_of(sy, sc), 2)
+
+    def half_of(sy):
+        return (sy % SIDE) // 2
+
+    mine = pair_rows(y, c)
+    swaps = {}
+    for e in ORDER:
+        theirs = pair_rows(y + e, 1 - c)
+        a = [send(part.at[:, half_of(y + e), first_half, theirs, :], a_swap.at[e, :, :, theirs, :], partner)]
+        b = []
         for h in range(2):
-            rows = pl.ds(pl.multiple_of(4 * h + 2 * c, 2), 2)
-            a_copies.append(send(
-                2 * (d - 1) + h,
-                both.at[pl.ds(2 * ((x + d) % SIDE), 2), pl.ds(0, HALF), rows, :],
-                a_got.at[d - 1, :, :, rows, :],
-                (rec_of(x + d, y, c), z),
-            ))
-    swaps[2].wait_recv()
-    swaps[3].wait_recv()
-    add_half(1)
-    b_copies = []
-    for d in (1, 2, 3):
-        rows = pl.ds(pair_of(y + d, c), 2)
+            rows = pl.ds(pl.multiple_of(4 * h + 2 * (1 - c), 2), 2)
+            b.append(send(part.at[(x + e) % SIDE, :, second_half, rows, :], b_swap.at[e, :, :, rows, :], partner))
+        swaps[e] = (a, b)
+    a_copies, b_copies = {}, {}
+    for e in ORDER:
+        for one in swaps[e][0]:
+            one.wait_recv()
         for s in range(SIDE):
-            b_copies.append(send(
-                6 + 4 * (d - 1) + s,
-                both.at[2 * s + ((y + d) % SIDE) // 2, pl.ds(HALF, HALF), rows, :],
-                b_got.at[d - 1, s, :, rows, :],
+            a_both[e, s] = part[s, half_of(y + e), first_half] + a_swap[e, s]
+        rows = pair_rows(y + e, c)
+        a_copies[e] = [
+            send(a_both.at[e, (x + d) % SIDE, :, rows, :], a_got.at[e, d - 1, :, rows, :], (rec_of(x + d, y, c), z))
+            for d in (2, 1, 3)
+        ]
+        for one in swaps[e][1]:
+            one.wait_recv()
+        for th in range(2):
+            b_both[e, th] = part[(x + e) % SIDE, th, second_half] + b_swap[e, th]
+        b_copies[e] = [
+            send(
+                b_both.at[e, half_of(y + d), :, pair_rows(y + d, c), :],
+                b_got.at[e, d - 1, :, pair_rows(y + d, c), :],
                 (rec_of(x, y + d, c), z),
-            ))
-    for one in a_copies:
-        one.wait_recv()
-    for th in range(2):
-        a_sum[th] = both[2 * x + th, pl.ds(0, HALF)] + a_got[0, th] + a_got[1, th] + a_got[2, th]
-    a_final = []
-    for d in (1, 2, 3):
-        rows = pl.ds(pair_of(y + d, c), 2)
-        a_final.append(send(
-            18 + d - 1, a_sum.at[((y + d) % SIDE) // 2, :, rows, :], a_last.at[d - 1, :, rows, :],
-            (rec_of(x, y + d, c), z),
-        ))
-    for one in b_copies:
-        one.wait_recv()
-    for s in range(SIDE):
-        b_sum[s] = both[2 * s + my_th, pl.ds(HALF, HALF)] + b_got[0, s] + b_got[1, s] + b_got[2, s]
-    b_final = []
-    for d in (1, 2, 3):
-        b_final.append(send(
-            21 + d - 1, b_sum.at[(x + d) % SIDE, :, my_pair, :], b_last.at[d - 1, :, my_pair, :],
-            (rec_of(x + d, y, c), z),
-        ))
+            )
+            for d in (2, 1, 3)
+        ]
+    a_final, b_final = [], []
+    for e in ORDER:
+        for one in a_copies[e]:
+            one.wait_recv()
+        a_total = a_both[e, x] + a_got[e, 0] + a_got[e, 1] + a_got[e, 2]
+        if e:
+            rows = pair_rows(y + e, c)
+            a_sum[e - 1] = a_total
+            a_final.append(
+                send(a_sum.at[e - 1, :, rows, :], a_last.at[e - 1, :, rows, :], (rec_of(x, y + e, c), z))
+            )
+        else:
+            done[first_half] = a_total
+        for one in b_copies[e]:
+            one.wait_recv()
+        b_total = b_both[e, half_of(y)] + b_got[e, 0] + b_got[e, 1] + b_got[e, 2]
+        if e:
+            b_sum[e - 1] = b_total
+            b_final.append(
+                send(b_sum.at[e - 1, :, mine, :], b_last.at[e - 1, :, mine, :], (rec_of(x + e, y, c), z))
+            )
+        else:
+            done[second_half] = b_total
     for one in a_final:
         one.wait_recv()
-    done[pl.ds(0, HALF)] = a_sum[my_th] + a_last[0] + a_last[1] + a_last[2]
+    done[first_half] = done[first_half] + a_last[0] + a_last[1] + a_last[2]
     for one in b_final:
         one.wait_recv()
-    done[pl.ds(HALF, HALF)] = b_sum[x] + b_last[0] + b_last[1] + b_last[2]
-    final = pltpu.make_async_copy(done.at[:, my_pair, :], out, l_sem)
+    done[second_half] = done[second_half] + b_last[0] + b_last[1] + b_last[2]
+    final = pltpu.make_async_copy(done.at[:, mine, :], out, l_sem)
     final.start()
-    for one in swaps + pending:
+    for one in pending:
         one.wait_send()
     final.wait()
 
@@ -382,23 +413,31 @@
     deviation, footprint, tile_list, offset, observed, obs_group, group_var, inv_time, inv_lat, inv_lon
 ):
     vmem = pl.BlockSpec(memory_space=pltpu.VMEM)
-    smem = pl.BlockSpec(memory_space=pltpu.SMEM)
-    hbm = pl.BlockSpec(memory_space=pl.ANY)
+    hbm = pl.BlockSpec(memory_space=pltpu.HBM)
     slots = jnp.transpose(tile_list, (1, 2, 0)).reshape(2, RECEPTORS)
     copies = 61
-    misfit_row, prior, lat = pl.pallas_call(
+    misfit_row, prior, lat, blocks = pl.pallas_call(
         forward_kernel,
         name="forward",
         out_shape=(
             jax.ShapeDtypeStruct((1, RECEPTORS), F32),
             jax.ShapeDtypeStruct((2 * PERIODS, 128), F32),
             jax.ShapeDtypeStruct((2, 64, 128), F32),
+            jax.ShapeDtypeStruct((RECEPTORS, 2, WINDOW, 8, 128), jnp.bfloat16),
         ),
-        in_specs=[smem, smem, smem, vmem, vmem, hbm, vmem, vmem, vmem, vmem, vmem],
-        out_specs=(vmem, vmem, vmem),
+        in_specs=[hbm] * 11,
+        out_specs=(vmem, vmem, vmem, vmem),
         scratch_shapes=[
+            pltpu.SMEM((2, RECEPTORS), jnp.int32),
+            pltpu.SMEM((RECEPTORS,), jnp.int32),
+            pltpu.SMEM((4,), F32),
+            pltpu.VMEM((1, RECEPTORS), F32),
+            pltpu.VMEM((1, RECEPTORS), jnp.int32),
+            pltpu.VMEM((PERIODS, PERIODS), F32),
+            pltpu.VMEM((64, 64), F32),
+            pltpu.VMEM((128, 1024), F32),
+            pltpu.SemaphoreType.DMA((8,)),
             pltpu.VMEM((ROWS, 8, 128), F32),
-            pltpu.VMEM((RECEPTORS, 2, WINDOW, 8, 128), jnp.bfloat16),
             pltpu.VMEM((RECEPTORS, 128), F32),
             pltpu.VMEM((STRIPS, 2 * PERIODS, 128), F32),
             pltpu.VMEM((STRIPS, RECEPTORS), F32),
@@ -414,55 +453,65 @@
         ],
         compiler_params=pltpu.CompilerParams(collective_id=0, has_side_effects=True, vmem_limit_bytes=VMEM_LIMIT),
     )(
-        slots,
-        offset,
-        group_var,
-        deviation,
-        deviation.reshape(2 * PERIODS, 128),
-        footprint,
-        observed.reshape(1, RECEPTORS),
-        obs_group.reshape(1, RECEPTORS),
-        inv_time,
-        inv_lat,
-        inv_lon,
+        *map(in_hbm, (
+            slots,
+            offset,
+            group_var,
+            deviation,
+            deviation.reshape(2 * PERIODS, 128),
+            footprint,
+            observed.reshape(1, RECEPTORS),
+            obs_group.reshape(1, RECEPTORS),
+            inv_time,
+            inv_lat,
+            inv_lon,
+        ))
     )
-    total, misfit = pl.pallas_call(
+    total, second, misfit = pl.pallas_call(
         adjoint_kernel,
         name="adjoint",
-        out_shape=(jax.ShapeDtypeStruct((ROWS, 8, 128), F32), jax.ShapeDtypeStruct((1, RECEPTORS), F32)),
-        in_specs=[smem, smem, smem, hbm, vmem, vmem, vmem],
-        out_specs=(vmem, vmem),
+        out_shape=(
+            jax.ShapeDtypeStruct((SUM_ROWS, 8, 128), F32),
+            jax.ShapeDtypeStruct((SUM_ROWS, 8, 128), F32),
+            jax.ShapeDtypeStruct((1, RECEPTORS), F32),
+        ),
+        in_specs=[hbm, hbm, pl.BlockSpec(memory_space=pl.ANY), vmem, vmem],
+        out_specs=(vmem, vmem, vmem),
         scratch_shapes=[
-            pltpu.VMEM((RECEPTORS, 2, WINDOW, 8, 128), jnp.bfloat16),
-            pltpu.VMEM((ROWS, 8, 128), F32),
-            pltpu.SemaphoreType.DMA((CHUNKS,)),
+            pltpu.SMEM((2, RECEPTORS), jnp.int32),
+            pltpu.SMEM((RECEPTORS,), jnp.int32),
+            pltpu.SMEM((RECEPTORS,), F32),
+            pltpu.SemaphoreType.DMA((3,)),
         ],
         compiler_params=pltpu.CompilerParams(vmem_limit_bytes=VMEM_LIMIT),
-    )(slots, offset, misfit_row.reshape(RECEPTORS), footprint, prior, lat, misfit_row)
+    )(in_hbm(slots), in_hbm(offset), misfit_row.reshape(RECEPTORS), blocks, misfit_row)
+    piece = (HALF, 8, 128)
+    shape = (TILES // 2 + 1, 2, PERIODS, 8, 128)
     gradient = pl.pallas_call(
         scatter_kernel,
         name="scatter",
         out_shape=jax.ShapeDtypeStruct((PERIODS, 2, 128), F32),
-        in_specs=[vmem],
+        in_specs=[vmem] * 4,
         out_specs=hbm,
         scratch_shapes=[
-            pltpu.VMEM((TILES, PERIODS, 8, 128), F32),
-            pltpu.VMEM((TILES, PERIODS, 8, 128), F32),
-            pltpu.VMEM((3, 2, HALF, 8, 128), F32),
-            pltpu.VMEM((2, HALF, 8, 128), F32),
-            pltpu.VMEM((3, HALF, 8, 128), F32),
-            pltpu.VMEM((3, SIDE, HALF, 8, 128), F32),
-            pltpu.VMEM((SIDE, HALF, 8, 128), F32),
-            pltpu.VMEM((3, HALF, 8, 128), F32),
+            pltpu.VMEM((SIDE, 2, PERIODS, 8, 128), F32),
+            pltpu.VMEM((4, SIDE, *piece), F32),
+            pltpu.VMEM((4, SIDE, *piece), F32),
+            pltpu.VMEM((4, 3, *piece), F32),
+            pltpu.VMEM((3, *piece), F32),
+            pltpu.VMEM((3, *piece), F32),
+            pltpu.VMEM((4, 2, *piece), F32),
+            pltpu.VMEM((4, 2, *piece), F32),
+            pltpu.VMEM((4, 3, *piece), F32),
+            pltpu.VMEM((3, *piece), F32),
+            pltpu.VMEM((3, *piece), F32),
             pltpu.VMEM((PERIODS, 8, 128), F32),
-            pltpu.SemaphoreType.DMA((4,)),
-            pltpu.SemaphoreType.DMA((4,)),
-            pltpu.SemaphoreType.DMA((24,)),
-            pltpu.SemaphoreType.DMA((24,)),
+            pltpu.SemaphoreType.DMA((42,)),
+            pltpu.SemaphoreType.DMA((42,)),
             pltpu.SemaphoreType.DMA,
         ],
         compiler_params=pltpu.CompilerParams(collective_id=1, has_side_effects=True, vmem_limit_bytes=VMEM_LIMIT),
-    )(total.reshape(TILES + 1, PERIODS, 8, 128))
+    )(total.reshape(shape), second.reshape(shape), prior, lat)
     return gradient, misfit.reshape(RECEPTORS)
 
 

time: 59.3 us -> 47.7 us (0.80)
  local copies, waits for them, and re-layouts: 7.39 us -> 0.63 us
  Pallas kernels: 50.9 us -> 46.3 us
    unnamed x19 -> x1, local copies, waits for them, and re-layouts: 7.39 us -> 0.63 us
    pallas_call x1, Pallas kernels: 16.3 us -> 13.2 us  [shards(): pl.pallas_call(scatter_kernel, name='scatter', out_shape=jax.ShapeDtypeSt...]
    pallas_call x1, Pallas kernels: 5.37 us -> 3.94 us  [shards(): pl.pallas_call(adjoint_kernel, name='adjoint', out_shape=(jax.ShapeDtypeS...]
where the time goes in v2:
time: 47.7 us; the launch traced here: 47.5 us
  Pallas kernels  46.3 us (97%)
  between operations  0.66 us (1%)
  local copies, waits for them, and re-layouts  0.63 us (1%)
    pallas_call x1, Pallas kernels, shards(): pl.pallas_call(forward_kernel, name='forward', out_shape=(jax.ShapeDtypeS...  29.1 us
    pallas_call x1, Pallas kernels, shards(): pl.pallas_call(scatter_kernel, name='scatter', out_shape=jax.ShapeDtypeSt...  13.2 us
    pallas_call x1, Pallas kernels, shards(): pl.pallas_call(adjoint_kernel, name='adjoint', out_shape=(jax.ShapeDtypeS...  3.94 us

profile of v2, /device:TPU:1, one launch (start us, length us, event | category | flops | bytes accessed | tf_op | source)
XLA Modules:
  0.0 47.5 jit_solution(13342829788905441285)
XLA Ops:
  0.6 29.1 %forward.1 = (f32[1,256]{1,0:T(1,128)S(1)}, f32[128,128]{1,0:T(8,128)S(1)}, f32[2,64,128]{2,1,0:T(8,128)S(1)}, bf16[256,2,8,8,128]{4,3,2,1,0:T(8,128)(2,1)S(1)}) custom-call(s32[2,256]{1,0:T(2,128)} %bitcast.14, s32[256]{0:T(256)} %starts_hbm.3, f32[4]{0:T(128)} %group_var_hbm.1, f32[64,2,128]{2,1,0:T(2,128)} %dev.1, f32[128,128]{1,0:T(8,128)} %bitcast.13, ...), custom_call_target="tpu_custom_call" | custom-call | tf_op jit(solution)/shard_map/forward/pallas_call | solution.py:419
  29.7 3.9 %adjoint.1 = (f32[640,8,128]{2,1,0:T(8,128)S(1)}, f32[640,8,128]{2,1,0:T(8,128)S(1)}, f32[1,256]{1,0:T(1,128)}) custom-call(s32[2,256]{1,0:T(2,128)} %bitcast.15, s32[256]{0:T(256)} %starts_hbm.3, f32[256]{0:T(256)S(1)} %bitcast.12, bf16[256,2,8,8,128]{4,3,2,1,0:T(8,128)(2,1)S(1)} %get-tuple-element.10.blocks, f32[1,256]{1,0:T(1,128)S(1)} %get-tuple-element.9.misfit_row), custom_call_target="tpu_custom_call" | custom-call | tf_op jit(solution)/shard_map/adjoint/pallas_call | solution.py:470
  33.7 13.2 %scatter.1 = f32[64,2,128]{2,1,0:T(2,128)S(1)} custom-call(f32[5,2,64,8,128]{4,3,2,1,0:T(8,128)S(1)} %bitcast.10, f32[5,2,64,8,128]{4,3,2,1,0:T(8,128)S(1)} %bitcast.11, f32[128,128]{1,0:T(8,128)S(1)} %get-tuple-element.13.prior, f32[2,64,128]{2,1,0:T(8,128)S(1)} %get-tuple-element.14.lat), custom_call_target="tpu_custom_call" | custom-call | tf_op jit(solution)/shard_map/scatter/pallas_call | solution.py:490
  46.9 0.6 %copy.13 = f32[64,2,128]{2,1,0:T(2,128)} copy(f32[64,2,128]{2,1,0:T(2,128)S(1)} %scatter.1) | data formatting | bytes 131072

commit v3 on v2

v3 whole, which is shorter than its diff:
```python
import functools

import jax
import jax.numpy as jnp
from jax import lax
from jax.experimental import pallas as pl
from jax.experimental.pallas import tpu as pltpu
from jax.sharding import PartitionSpec as P

MESH = pl.DeviceIdType.MESH
HIGHEST = lax.Precision.HIGHEST
F32 = jnp.float32
VMEM_LIMIT = 28 << 20

SIDE = 4
CORES = 2
PERIODS = 64
HALF = 32
WINDOW = 8
TILES = 8
ROWS = (TILES + 1) * PERIODS
SUM_ROWS = (TILES + 2) * PERIODS
RECEPTORS = 256
STRIPS = 8
GROUP = 8
UNROLL = 4
Z_NEAR = (2, 6, 1, 7)
Z_FAR = (4, 3, 5)
SENT_ROWS = 60 * 8 + 16
FAR_FIRST = (2, 1, 3)
NEAR_FIRST = (1, 3, 2)


def place():
    rec = lax.axis_index("rec")
    return rec // 8, (rec // 2) % SIDE, rec % 2, lax.axis_index("tile")


def rec_of(x, y, c):
    return ((x % SIDE) * SIDE + (y % SIDE)) * CORES + c


def tile_of(x, y):
    return 2 * (x % SIDE) + (y % SIDE) // 2


def pair_of(y, c):
    return pl.multiple_of(4 * ((y % SIDE) % 2) + 2 * c, 2)


def in_hbm(value):
    return pltpu.with_memory_space_constraint(value, pltpu.HBM)


def greet(peers):
    barrier = pltpu.get_barrier_semaphore()
    for peer in peers:
        pl.semaphore_signal(barrier, inc=1, device_id=peer, device_id_type=MESH)
    return barrier


def plane_peers(x, y, c, z):
    peers = [(rec_of(x, y, 1 - c), z)]
    peers += [(rec_of(x + d, y, c), z) for d in (1, 2, 3)]
    peers += [(rec_of(x, y + d, c), z) for d in (1, 2, 3)]
    return peers


def copy_to(src, dst, send, recv, peer):
    return pltpu.make_async_remote_copy(
        src_ref=src, dst_ref=dst, send_sem=send, recv_sem=recv, device_id=peer, device_id_type=MESH
    )


def forward_kernel(
    slots_hbm,
    starts_hbm,
    group_var_hbm,
    dev,
    dev_rows,
    foot,
    observed_hbm,
    group_hbm,
    inv_time_hbm,
    inv_lat_hbm,
    inv_lon_hbm,
    misfit_out,
    prior_out,
    lat_out,
    packed,
    slots,
    starts,
    group_var,
    observed,
    group,
    inv_time,
    inv_lat,
    inv_lon,
    i_sem,
    strip,
    sums,
    field,
    shares,
    own_share,
    send_sem,
    recv_sem,
    near_sem,
    token,
    z_send,
    z_recv,
    s_send,
    s_recv,
    f_sem,
    l_sem,
):
    x, y, c, z = place()
    me = rec_of(x, y, c)
    partner = (rec_of(x, y, 1 - c), z)
    peers = plane_peers(x, y, c, z) + [(me, (z + d) % STRIPS) for d in Z_NEAR]
    barrier = greet(peers)
    load_all = pltpu.make_async_copy(foot.at[:, 0], packed, f_sem)
    load_all.start()
    small = []
    for n, (src, dst) in enumerate((
        (inv_time_hbm, inv_time), (inv_lat_hbm, inv_lat), (slots_hbm, slots), (starts_hbm, starts),
        (group_var_hbm, group_var), (observed_hbm, observed), (group_hbm, group), (inv_lon_hbm, inv_lon),
    )):
        load = pltpu.make_async_copy(src, dst, i_sem.at[n])
        load.start()
        small.append(load)

    def spot(sx, sy, sc, first, count):
        return strip.at[
            pl.ds(pl.multiple_of(PERIODS * (1 + tile_of(sx, sy)) + first, HALF), count), pl.ds(pair_of(sy, sc), 2), :
        ]

    own_local = pltpu.make_async_copy(dev, spot(x, y, c, 0, PERIODS), l_sem.at[0])
    own_local.start()
    own_field = pltpu.make_async_copy(dev_rows, field.at[z], l_sem.at[1])
    own_field.start()
    pl.semaphore_wait(barrier, len(peers))
    for n, d in enumerate((2, STRIPS - 2)):
        pl.semaphore_signal(token.at[n], inc=1, device_id=(me, (z + d) % STRIPS), device_id_type=MESH)

    count = [0]

    def send(src, where, peer):
        n = count[0]
        count[0] += 1
        copy_to(src, where, send_sem, recv_sem.at[n], peer).start()
        return n

    def share_with_partner(src, where):
        copy_to(src, where, send_sem, near_sem, partner).start()

    def arrived(n, where):
        copy_to(where, where, send_sem, recv_sem.at[n], partner).wait_recv()

    first_a, first_b = dev.at[pl.ds(0, HALF)], dev.at[pl.ds(HALF, HALF)]
    in_a, in_b, far_a, far_b = {}, {}, {}, {}
    for d in FAR_FIRST:
        in_a[d] = send(first_a, spot(x, y, c, 0, HALF), (rec_of(x + d, y, c), z))
        in_b[d] = send(first_b, spot(x, y, c, HALF, HALF), (rec_of(x, y + d, c), z))
    for d in FAR_FIRST:
        far_a[0, d] = send(first_a, spot(x, y, c, 0, HALF), (rec_of(x, y + d, c), z))
        far_b[0, d] = send(first_b, spot(x, y, c, HALF, HALF), (rec_of(x + d, y, c), z))
    share_with_partner(dev, spot(x, y, c, 0, PERIODS))

    def send_along(d):
        copy_to(dev_rows, field.at[z], z_send, z_recv, (me, (z + d) % STRIPS)).start()

    for d in Z_NEAR:
        send_along(d)

    strip[pl.ds(0, PERIODS)] = jnp.zeros((PERIODS, 8, 128), F32)
    for load in small:
        load.wait()

    wide = (lax.broadcasted_iota(jnp.int32, (2 * PERIODS, PERIODS), 0) // 2
            == lax.broadcasted_iota(jnp.int32, (2 * PERIODS, PERIODS), 1)).astype(F32)
    time_rows = jnp.dot(wide, inv_time[...], precision=HIGHEST, preferred_element_type=F32)
    time_both = lax.dot_general(time_rows, wide, (((1,), (1,)), ((), ())), precision=HIGHEST, preferred_element_type=F32)
    square = (2 * PERIODS, 2 * PERIODS)
    same = lax.broadcasted_iota(jnp.int32, square, 0) % 2 == lax.broadcasted_iota(jnp.int32, square, 1) % 2
    time_both = jnp.where(same, time_both, 0.0)
    for n in range(2):
        pick = (lax.broadcasted_iota(jnp.int32, (64, 128), 0) == 2 * me + n).astype(F32)
        lat_out[n] = jnp.dot(inv_lat[...], pick, precision=HIGHEST, preferred_element_type=F32)

    for m in range(2):
        pl.semaphore_wait(token.at[m], 1)
    for d in Z_FAR:
        send_along(d)

    for d in NEAR_FIRST:
        here = spot(x - d, y, c, 0, HALF)
        arrived(in_a[d], here)
        for e in FAR_FIRST:
            far_a[d, e] = send(here, here, (rec_of(x, y + e, c), z))
        share_with_partner(here, here)
        here = spot(x, y - d, c, HALF, HALF)
        arrived(in_b[d], here)
        for e in FAR_FIRST:
            far_b[d, e] = send(here, here, (rec_of(x + e, y, c), z))
        share_with_partner(here, here)
    for d in (0, *NEAR_FIRST):
        for e in NEAR_FIRST:
            here = spot(x - d, y - e, c, 0, HALF)
            arrived(far_a[d, e], here)
            share_with_partner(here, here)
            here = spot(x - e, y - d, c, HALF, HALF)
            arrived(far_b[d, e], here)
            share_with_partner(here, here)
    half_strip = strip.at[pl.ds(0, TILES * PERIODS // 2)]
    copy_to(half_strip, half_strip, send_sem, near_sem, partner).wait_recv()
    own_local.wait()
    load_all.wait()

    def group_sums(block, i, carry):
        totals = []
        for u in range(GROUP):
            r = block * 128 + i * GROUP + u
            start = starts[r]
            parts = []
            for k in range(2):
                base = (slots[block, k, i * GROUP + u] + 1) * PERIODS + start
                parts.append(strip[pl.ds(base, WINDOW)] * packed[r, k].astype(F32))
            totals.append(jnp.sum(parts[0] + parts[1], axis=0))
        sums[pl.ds(pl.multiple_of(block * 128 + i * GROUP, GROUP), GROUP), :] = jnp.sum(jnp.stack(totals), axis=1)
        return carry

    for block in range(2):
        lax.fori_loop(0, 128 // GROUP, functools.partial(group_sums, block), 0)
    share = lax.dot_general(
        jnp.ones((8, 128), F32), sums[...], (((1,), (1,)), ((), ())), precision=HIGHEST, preferred_element_type=F32
    )
    own_share[...] = share
    for d in Z_FAR + Z_NEAR:
        copy_to(
            own_share.at[pl.ds(0, 1), :], shares.at[pl.ds(z, 1), :], s_send, s_recv, (me, (z + d) % STRIPS)
        ).start()
    mine = pltpu.make_async_copy(own_share.at[pl.ds(0, 1), :], shares.at[pl.ds(z, 1), :], l_sem.at[2])
    mine.start()

    own_field.wait()
    others = field.at[pl.ds(0, STRIPS - 1)]
    copy_to(others, others, z_send, z_recv, partner).wait()
    lon_done = jnp.zeros((2 * PERIODS, 128), F32)
    for s in range(STRIPS):
        lon_done += lax.dot_general(
            field[s], inv_lon[:, s * 128 : (s + 1) * 128], (((1,), (1,)), ((), ())),
            precision=HIGHEST, preferred_element_type=F32,
        )
    prior_out[...] = jnp.dot(time_both, lon_done, precision=HIGHEST, preferred_element_type=F32)

    mine.wait()
    sent = strip.at[pl.ds(0, SENT_ROWS)]
    copy_to(sent, sent, send_sem, near_sem, partner).wait_send()
    others = shares.at[pl.ds(0, STRIPS - 1), :]
    copy_to(others, others, s_send, s_recv, partner).wait()
    predicted = jnp.sum(shares[...], axis=0, keepdims=True)
    variance = jnp.zeros((1, RECEPTORS), F32)
    for g in range(4):
        variance += jnp.where(group[...] == g, group_var[g], 0.0)
    misfit_out[...] = (predicted - observed[...]) / variance


def adjoint_kernel(
    slots_hbm, starts_hbm, misfit_hbm, blocks, misfit_row, total, second, misfit_out, slots, starts, misfit, i_sem
):
    small = []
    for n, (src, dst) in enumerate(((slots_hbm, slots), (starts_hbm, starts), (misfit_hbm, misfit))):
        load = pltpu.make_async_copy(src, dst, i_sem.at[n])
        load.start()
        small.append(load)
    misfit_out[...] = misfit_row[...]

    def clear(i, carry):
        rows = pl.ds(pl.multiple_of(i * 16, 16), 16)
        total[rows] = jnp.zeros((16, 8, 128), F32)
        second[rows] = jnp.zeros((16, 8, 128), F32)
        return carry

    lax.fori_loop(0, SUM_ROWS // 16, clear, 0)
    for load in small:
        load.wait()

    def pair(block, i, carry):
        held = []
        for u, into in ((0, total), (1, second)):
            r = block * 128 + 2 * i + u
            start = starts[r]
            weight = misfit[r]
            for k in range(2):
                rows = pl.ds((slots[block, k, 2 * i + u] + 2) * PERIODS + start, WINDOW)
                held.append((into, rows, into[rows] + blocks[r, k].astype(F32) * weight))
        for into, rows, value in held:
            into[rows] = value
        return carry

    for block in range(2):
        lax.fori_loop(0, 64, functools.partial(pair, block), 0, unroll=UNROLL)


ORDER = (2, 1, 3, 0)


def scatter_kernel(
    total, second, prior, lat, out, part, a_swap, a_both, a_got, a_sum, a_last, b_swap, b_both, b_got, b_sum, b_last,
    done, send_sem, recv_sem,
):
    x, y, c, z = place()
    partner = (rec_of(x, y, 1 - c), z)
    peers = plane_peers(x, y, c, z)
    barrier = greet(peers)

    def one_period(p, carry):
        first = jnp.broadcast_to(prior[pl.ds(2 * p, 1), :], (8, 128))
        other = jnp.broadcast_to(prior[pl.ds(2 * p + 1, 1), :], (8, 128))
        for t in range(TILES):
            rows = slice(8 * t, 8 * t + 8)
            part[t // 2, t % 2, p] = (
                total[1 + t // 2, t % 2, p] + second[1 + t // 2, t % 2, p]
                + (lat[0, rows, :] * first + lat[1, rows, :] * other)
            )
        return carry

    lax.fori_loop(0, PERIODS, one_period, 0)
    pl.semaphore_wait(barrier, len(peers))

    first_half, second_half = pl.ds(0, HALF), pl.ds(HALF, HALF)
    def send(n, src, dst, peer):
        copy_to(src, dst, send_sem, recv_sem.at[n], peer).start()

    def arrived(n, where):
        copy_to(where, where, send_sem, recv_sem.at[n], partner).wait_recv()

    def pair_rows(sy, sc):
        return pl.ds(pair_of(sy, sc), 2)

    def half_of(sy):
        return (sy % SIDE) // 2

    mine = pair_rows(y, c)
    for e in ORDER:
        theirs = pair_rows(y + e, 1 - c)
        send(e, part.at[:, half_of(y + e), first_half, theirs, :], a_swap.at[e, :, :, theirs, :], partner)
        for h in range(2):
            rows = pl.ds(pl.multiple_of(4 * h + 2 * (1 - c), 2), 2)
            send(4 + e, part.at[(x + e) % SIDE, :, second_half, rows, :], b_swap.at[e, :, :, rows, :], partner)
    for e in ORDER:
        rows = pair_rows(y + e, c)
        arrived(e, a_swap.at[e, :, :, rows, :])
        for s in range(SIDE):
            a_both[e, s] = part[s, half_of(y + e), first_half] + a_swap[e, s]
        for d in FAR_FIRST:
            send(
                8 + e, a_both.at[e, (x + d) % SIDE, :, rows, :], a_got.at[e, d - 1, :, rows, :], (rec_of(x + d, y, c), z)
            )
        both_rows = b_swap.at[e, :, :, pl.ds(0, 4), :]
        arrived(4 + e, both_rows)
        for th in range(2):
            b_both[e, th] = part[(x + e) % SIDE, th, second_half] + b_swap[e, th]
        for d in FAR_FIRST:
            send(
                12 + e,
                b_both.at[e, half_of(y + d), :, pair_rows(y + d, c), :],
                b_got.at[e, d - 1, :, pair_rows(y + d, c), :],
                (rec_of(x, y + d, c), z),
            )
    for e in ORDER:
        rows = pair_rows(y + e, c)
        arrived(8 + e, a_got.at[e, :, :, rows, :])
        a_total = a_both[e, x] + a_got[e, 0] + a_got[e, 1] + a_got[e, 2]
        if e:
            a_sum[e - 1] = a_total
            send(16, a_sum.at[e - 1, :, rows, :], a_last.at[e - 1, :, rows, :], (rec_of(x, y + e, c), z))
        else:
            done[first_half] = a_total
        arrived(12 + e, b_got.at[e, :, :, mine, :])
        b_total = b_both[e, half_of(y)] + b_got[e, 0] + b_got[e, 1] + b_got[e, 2]
        if e:
            b_sum[e - 1] = b_total
            send(17, b_sum.at[e - 1, :, mine, :], b_last.at[e - 1, :, mine, :], (rec_of(x + e, y, c), z))
        else:
            done[second_half] = b_total
    sent = total.at[pl.ds(0, 4), :, pl.ds(0, 62), :, :]
    copy_to(sent, sent, send_sem, recv_sem.at[0], partner).wait_send()
    arrived(16, a_last.at[:, :, mine, :])
    out[first_half] = (
        done[first_half, mine, :] + a_last[0, :, mine, :] + a_last[1, :, mine, :] + a_last[2, :, mine, :]
    )
    arrived(17, b_last.at[:, :, mine, :])
    out[second_half] = (
        done[second_half, mine, :] + b_last[0, :, mine, :] + b_last[1, :, mine, :] + b_last[2, :, mine, :]
    )


def shards(
    deviation, footprint, tile_list, offset, observed, obs_group, group_var, inv_time, inv_lat, inv_lon
):
    vmem = pl.BlockSpec(memory_space=pltpu.VMEM)
    hbm = pl.BlockSpec(memory_space=pltpu.HBM)
    slots = jnp.transpose(tile_list.reshape(2, 128, 2), (0, 2, 1))
    misfit_row, prior, lat, packed = pl.pallas_call(
        forward_kernel,
        name="forward",
        out_shape=(
            jax.ShapeDtypeStruct((1, RECEPTORS), F32),
            jax.ShapeDtypeStruct((2 * PERIODS, 128), F32),
            jax.ShapeDtypeStruct((2, 64, 128), F32),
            jax.ShapeDtypeStruct((RECEPTORS, 2, WINDOW, 8, 128), jnp.bfloat16),
        ),
        in_specs=[hbm] * 11,
        out_specs=(vmem, vmem, vmem, vmem),
        scratch_shapes=[
            pltpu.SMEM((2, 2, 128), jnp.int32),
            pltpu.SMEM((RECEPTORS,), jnp.int32),
            pltpu.SMEM((4,), F32),
            pltpu.VMEM((1, RECEPTORS), F32),
            pltpu.VMEM((1, RECEPTORS), jnp.int32),
            pltpu.VMEM((PERIODS, PERIODS), F32),
            pltpu.VMEM((64, 64), F32),
            pltpu.VMEM((128, 1024), F32),
            pltpu.SemaphoreType.DMA((8,)),
            pltpu.VMEM((ROWS, 8, 128), F32),
            pltpu.VMEM((RECEPTORS, 128), F32),
            pltpu.VMEM((STRIPS, 2 * PERIODS, 128), F32),
            pltpu.VMEM((STRIPS, RECEPTORS), F32),
            pltpu.VMEM((8, RECEPTORS), F32),
            pltpu.SemaphoreType.DMA,
            pltpu.SemaphoreType.DMA((30,)),
            pltpu.SemaphoreType.DMA,
            pltpu.SemaphoreType.REGULAR((2,)),
            pltpu.SemaphoreType.DMA,
            pltpu.SemaphoreType.DMA,
            pltpu.SemaphoreType.DMA,
            pltpu.SemaphoreType.DMA,
            pltpu.SemaphoreType.DMA,
            pltpu.SemaphoreType.DMA((3,)),
        ],
        compiler_params=pltpu.CompilerParams(collective_id=0, has_side_effects=True, vmem_limit_bytes=VMEM_LIMIT),
    )(
        *map(in_hbm, (
            slots,
            offset,
            group_var,
            deviation,
            deviation.reshape(2 * PERIODS, 128),
            footprint,
            observed.reshape(1, RECEPTORS),
            obs_group.reshape(1, RECEPTORS),
            inv_time,
            inv_lat,
            inv_lon,
        ))
    )
    total, second, misfit = pl.pallas_call(
        adjoint_kernel,
        name="adjoint",
        out_shape=(
            jax.ShapeDtypeStruct((SUM_ROWS, 8, 128), F32),
            jax.ShapeDtypeStruct((SUM_ROWS, 8, 128), F32),
            jax.ShapeDtypeStruct((1, RECEPTORS), F32),
        ),
        in_specs=[hbm, hbm, pl.BlockSpec(memory_space=pl.ANY), vmem, vmem],
        out_specs=(vmem, vmem, vmem),
        scratch_shapes=[
            pltpu.SMEM((2, 2, 128), jnp.int32),
            pltpu.SMEM((RECEPTORS,), jnp.int32),
            pltpu.SMEM((RECEPTORS,), F32),
            pltpu.SemaphoreType.DMA((3,)),
        ],
        compiler_params=pltpu.CompilerParams(vmem_limit_bytes=VMEM_LIMIT),
    )(in_hbm(slots), in_hbm(offset), misfit_row.reshape(RECEPTORS), packed, misfit_row)
    piece = (HALF, 8, 128)
    shape = (TILES // 2 + 1, 2, PERIODS, 8, 128)
    gradient = pl.pallas_call(
        scatter_kernel,
        name="scatter",
        out_shape=jax.ShapeDtypeStruct((PERIODS, 2, 128), F32),
        in_specs=[vmem] * 4,
        out_specs=vmem,
        scratch_shapes=[
            pltpu.VMEM((SIDE, 2, PERIODS, 8, 128), F32),
            pltpu.VMEM((4, SIDE, *piece), F32),
            pltpu.VMEM((4, SIDE, *piece), F32),
            pltpu.VMEM((4, 3, *piece), F32),
            pltpu.VMEM((3, *piece), F32),
            pltpu.VMEM((3, *piece), F32),
            pltpu.VMEM((4, 2, *piece), F32),
            pltpu.VMEM((4, 2, *piece), F32),
            pltpu.VMEM((4, 3, *piece), F32),
            pltpu.VMEM((3, *piece), F32),
            pltpu.VMEM((3, *piece), F32),
            pltpu.VMEM((PERIODS, 8, 128), F32),
            pltpu.SemaphoreType.DMA,
            pltpu.SemaphoreType.DMA((18,)),
        ],
        compiler_params=pltpu.CompilerParams(collective_id=1, has_side_effects=True, vmem_limit_bytes=VMEM_LIMIT),
    )(total.reshape(shape), second.reshape(shape), prior, lat)
    return gradient, misfit.reshape(RECEPTORS)


def solution(mesh):
    return jax.shard_map(
        shards,
        mesh=mesh,
        in_specs=(
            P(None, "rec", "tile"),
            P("rec", "tile", None, None, None, None),
            P("rec", "tile", None),
            P("rec"),
            P("rec"),
            P("rec"),
            P(),
            P(),
            P(),
            P("tile", None),
        ),
        out_specs=(P(None, "rec", "tile"), P("rec")),
        check_vma=False,
    )
```

time: 47.7 us -> 44.3 us (0.929)
  Pallas kernels: 46.3 us -> 42.9 us
    pallas_call x1, Pallas kernels: 29.1 us -> 27.5 us  [shards(): pl.pallas_call(forward_kernel, name='forward', out_shape=(jax.ShapeDtypeS...]
    pallas_call x1, Pallas kernels: 13.2 us -> 12.2 us  [shards(): pl.pallas_call(scatter_kernel, name='scatter', out_shape=jax.ShapeDtypeSt...]
    pallas_call x1, Pallas kernels: 3.94 us -> 3.18 us  [shards(): pl.pallas_call(adjoint_kernel, name='adjoint', out_shape=(jax.ShapeDtypeS...]
where the time goes in v3:
time: 44.3 us; the launch traced here: 44.2 us
  Pallas kernels  42.9 us (97%)
  between operations  0.66 us (1%)
  local copies, waits for them, and re-layouts  0.63 us (1%)
    pallas_call x1, Pallas kernels, shards(): pl.pallas_call(forward_kernel, name='forward', out_shape=(jax.ShapeDtypeS...  27.5 us
    pallas_call x1, Pallas kernels, shards(): pl.pallas_call(scatter_kernel, name='scatter', out_shape=jax.ShapeDtypeSt...  12.2 us
    pallas_call x1, Pallas kernels, shards(): pl.pallas_call(adjoint_kernel, name='adjoint', out_shape=(jax.ShapeDtypeS...  3.18 us

profile of v3, /device:TPU:1, one launch (start us, length us, event | category | flops | bytes accessed | tf_op | source)
XLA Modules:
  0.0 44.2 jit_solution(11610404984266022190)
XLA Ops:
  0.6 27.5 %forward.1 = (f32[1,256]{1,0:T(1,128)S(1)}, f32[128,128]{1,0:T(8,128)S(1)}, f32[2,64,128]{2,1,0:T(8,128)S(1)}, bf16[256,2,8,8,128]{4,3,2,1,0:T(8,128)(2,1)S(1)}) custom-call(s32[2,2,128]{2,1,0:T(2,128)} %bitcast.14, s32[256]{0:T(256)} %starts_hbm.3, f32[4]{0:T(128)} %group_var_hbm.1, f32[64,2,128]{2,1,0:T(2,128)} %dev.1, f32[128,128]{1,0:T(8,128)} %bitcast.13, ...), custom_call_target="tpu_custom_call" | custom-call | tf_op jit(solution)/shard_map/forward/pallas_call | solution.py:405
  28.2 3.2 %adjoint.1 = (f32[640,8,128]{2,1,0:T(8,128)S(1)}, f32[640,8,128]{2,1,0:T(8,128)S(1)}, f32[1,256]{1,0:T(1,128)}) custom-call(s32[2,2,128]{2,1,0:T(2,128)} %bitcast.15, s32[256]{0:T(256)} %starts_hbm.3, f32[256]{0:T(256)S(1)} %bitcast.12, bf16[256,2,8,8,128]{4,3,2,1,0:T(8,128)(2,1)S(1)} %get-tuple-element.10.blocks, f32[1,256]{1,0:T(1,128)S(1)} %get-tuple-element.9.misfit_row), custom_call_target="tpu_custom_call" | custom-call | tf_op jit(solution)/shard_map/adjoint/pallas_call | solution.py:458
  31.4 12.2 %scatter.1 = f32[64,2,128]{2,1,0:T(2,128)S(1)} custom-call(f32[5,2,64,8,128]{4,3,2,1,0:T(8,128)S(1)} %bitcast.10, f32[5,2,64,8,128]{4,3,2,1,0:T(8,128)S(1)} %bitcast.11, f32[128,128]{1,0:T(8,128)S(1)} %get-tuple-element.13.prior, f32[2,64,128]{2,1,0:T(8,128)S(1)} %get-tuple-element.14.lat), custom_call_target="tpu_custom_call" | custom-call | tf_op jit(solution)/shard_map/scatter/pallas_call | solution.py:478
  43.6 0.6 %copy.13 = f32[64,2,128]{2,1,0:T(2,128)} copy(f32[64,2,128]{2,1,0:T(2,128)S(1)} %scatter.1) | data formatting | bytes 131072

commit v4 on v3

--- a/solution.py
+++ b/solution.py
@@ -23,7 +23,7 @@
 RECEPTORS = 256
 STRIPS = 8
 GROUP = 8
-UNROLL = 4
+UNROLL = 8
 Z_NEAR = (2, 6, 1, 7)
 Z_FAR = (4, 3, 5)
 SENT_ROWS = 60 * 8 + 16
@@ -88,6 +88,10 @@
     prior_out,
     lat_out,
     packed,
+    clear_one,
+    clear_two,
+    slots_out,
+    starts_out,
     slots,
     starts,
     group_var,
@@ -97,6 +101,8 @@
     inv_lat,
     inv_lon,
     i_sem,
+    firsts,
+    blocks,
     strip,
     sums,
     field,
@@ -118,26 +124,28 @@
     partner = (rec_of(x, y, 1 - c), z)
     peers = plane_peers(x, y, c, z) + [(me, (z + d) % STRIPS) for d in Z_NEAR]
     barrier = greet(peers)
+    def spot(sx, sy, sc, first, count):
+        return strip.at[
+            pl.ds(pl.multiple_of(PERIODS * (1 + tile_of(sx, sy)) + first, HALF), count), pl.ds(pair_of(sy, sc), 2), :
+        ]
+
+    own_local = pltpu.make_async_copy(dev, spot(x, y, c, 0, PERIODS), l_sem.at[0])
+    own_local.start()
     load_all = pltpu.make_async_copy(foot.at[:, 0], packed, f_sem)
     load_all.start()
     small = []
     for n, (src, dst) in enumerate((
         (inv_time_hbm, inv_time), (inv_lat_hbm, inv_lat), (slots_hbm, slots), (starts_hbm, starts),
         (group_var_hbm, group_var), (observed_hbm, observed), (group_hbm, group), (inv_lon_hbm, inv_lon),
+        (slots_hbm, slots_out), (starts_hbm, starts_out),
     )):
         load = pltpu.make_async_copy(src, dst, i_sem.at[n])
         load.start()
         small.append(load)
 
-    def spot(sx, sy, sc, first, count):
-        return strip.at[
-            pl.ds(pl.multiple_of(PERIODS * (1 + tile_of(sx, sy)) + first, HALF), count), pl.ds(pair_of(sy, sc), 2), :
-        ]
-
-    own_local = pltpu.make_async_copy(dev, spot(x, y, c, 0, PERIODS), l_sem.at[0])
-    own_local.start()
     own_field = pltpu.make_async_copy(dev_rows, field.at[z], l_sem.at[1])
     own_field.start()
+    own_local.wait()
     pl.semaphore_wait(barrier, len(peers))
     for n, d in enumerate((2, STRIPS - 2)):
         pl.semaphore_signal(token.at[n], inc=1, device_id=(me, (z + d) % STRIPS), device_id_type=MESH)
@@ -156,7 +164,8 @@
     def arrived(n, where):
         copy_to(where, where, send_sem, recv_sem.at[n], partner).wait_recv()
 
-    first_a, first_b = dev.at[pl.ds(0, HALF)], dev.at[pl.ds(HALF, HALF)]
+    first_a, first_b = spot(x, y, c, 0, HALF), spot(x, y, c, HALF, HALF)
+    first_both = spot(x, y, c, 0, PERIODS)
     in_a, in_b, far_a, far_b = {}, {}, {}, {}
     for d in FAR_FIRST:
         in_a[d] = send(first_a, spot(x, y, c, 0, HALF), (rec_of(x + d, y, c), z))
@@ -164,7 +173,7 @@
     for d in FAR_FIRST:
         far_a[0, d] = send(first_a, spot(x, y, c, 0, HALF), (rec_of(x, y + d, c), z))
         far_b[0, d] = send(first_b, spot(x, y, c, HALF, HALF), (rec_of(x + d, y, c), z))
-    share_with_partner(dev, spot(x, y, c, 0, PERIODS))
+    share_with_partner(first_both, first_both)
 
     def send_along(d):
         copy_to(dev_rows, field.at[z], z_send, z_recv, (me, (z + d) % STRIPS)).start()
@@ -203,6 +212,25 @@
         for e in FAR_FIRST:
             far_b[d, e] = send(here, here, (rec_of(x + e, y, c), z))
         share_with_partner(here, here)
+
+    def clear(i, carry):
+        rows = pl.ds(pl.multiple_of(i * 16, 16), 16)
+        clear_one[rows] = jnp.zeros((16, 8, 128), F32)
+        clear_two[rows] = jnp.zeros((16, 8, 128), F32)
+        return carry
+
+    lax.fori_loop(0, SUM_ROWS // 16, clear, 0)
+    load_all.wait()
+
+    def widen(block, i, carry):
+        r = block * 128 + i
+        blocks[r] = packed[r].astype(F32)
+        for k in range(2):
+            firsts[2 * r + k] = (slots[block, k, i] + 1) * PERIODS + starts[r]
+        return carry
+
+    for block in range(2):
+        lax.fori_loop(0, 128, functools.partial(widen, block), 0, unroll=4)
     for d in (0, *NEAR_FIRST):
         for e in NEAR_FIRST:
             here = spot(x - d, y - e, c, 0, HALF)
@@ -213,24 +241,21 @@
             share_with_partner(here, here)
     half_strip = strip.at[pl.ds(0, TILES * PERIODS // 2)]
     copy_to(half_strip, half_strip, send_sem, near_sem, partner).wait_recv()
-    own_local.wait()
-    load_all.wait()
 
     def group_sums(block, i, carry):
         totals = []
         for u in range(GROUP):
             r = block * 128 + i * GROUP + u
-            start = starts[r]
             parts = []
             for k in range(2):
-                base = (slots[block, k, i * GROUP + u] + 1) * PERIODS + start
-                parts.append(strip[pl.ds(base, WINDOW)] * packed[r, k].astype(F32))
+                base = firsts[2 * r + k]
+                parts.append(strip[pl.ds(base, WINDOW)] * blocks[r, k])
             totals.append(jnp.sum(parts[0] + parts[1], axis=0))
         sums[pl.ds(pl.multiple_of(block * 128 + i * GROUP, GROUP), GROUP), :] = jnp.sum(jnp.stack(totals), axis=1)
         return carry
 
     for block in range(2):
-        lax.fori_loop(0, 128 // GROUP, functools.partial(group_sums, block), 0)
+        lax.fori_loop(0, 128 // GROUP, functools.partial(group_sums, block), 0, unroll=2)
     share = lax.dot_general(
         jnp.ones((8, 128), F32), sums[...], (((1,), (1,)), ((), ())), precision=HIGHEST, preferred_element_type=F32
     )
@@ -266,22 +291,16 @@
 
 
 def adjoint_kernel(
-    slots_hbm, starts_hbm, misfit_hbm, blocks, misfit_row, total, second, misfit_out, slots, starts, misfit, i_sem
+    slots_hbm, starts_hbm, misfit_hbm, blocks, misfit_row, clear_one, clear_two, total, second, misfit_out, slots, starts, misfit, i_sem
 ):
     small = []
     for n, (src, dst) in enumerate(((slots_hbm, slots), (starts_hbm, starts), (misfit_hbm, misfit))):
         load = pltpu.make_async_copy(src, dst, i_sem.at[n])
         load.start()
         small.append(load)
-    misfit_out[...] = misfit_row[...]
-
-    def clear(i, carry):
-        rows = pl.ds(pl.multiple_of(i * 16, 16), 16)
-        total[rows] = jnp.zeros((16, 8, 128), F32)
-        second[rows] = jnp.zeros((16, 8, 128), F32)
-        return carry
-
-    lax.fori_loop(0, SUM_ROWS // 16, clear, 0)
+    result = pltpu.make_async_copy(misfit_row, misfit_out, i_sem.at[3])
+    result.start()
+
     for load in small:
         load.wait()
 
@@ -300,6 +319,7 @@
 
     for block in range(2):
         lax.fori_loop(0, 64, functools.partial(pair, block), 0, unroll=UNROLL)
+    result.wait()
 
 
 ORDER = (2, 1, 3, 0)
@@ -402,7 +422,7 @@
     vmem = pl.BlockSpec(memory_space=pltpu.VMEM)
     hbm = pl.BlockSpec(memory_space=pltpu.HBM)
     slots = jnp.transpose(tile_list.reshape(2, 128, 2), (0, 2, 1))
-    misfit_row, prior, lat, packed = pl.pallas_call(
+    misfit_row, prior, lat, packed, clear_one, clear_two, slots_near, starts_near = pl.pallas_call(
         forward_kernel,
         name="forward",
         out_shape=(
@@ -410,9 +430,13 @@
             jax.ShapeDtypeStruct((2 * PERIODS, 128), F32),
             jax.ShapeDtypeStruct((2, 64, 128), F32),
             jax.ShapeDtypeStruct((RECEPTORS, 2, WINDOW, 8, 128), jnp.bfloat16),
+            jax.ShapeDtypeStruct((SUM_ROWS, 8, 128), F32),
+            jax.ShapeDtypeStruct((SUM_ROWS, 8, 128), F32),
+            jax.ShapeDtypeStruct((2, 2, 128), jnp.int32),
+            jax.ShapeDtypeStruct((RECEPTORS,), jnp.int32),
         ),
         in_specs=[hbm] * 11,
-        out_specs=(vmem, vmem, vmem, vmem),
+        out_specs=(vmem,) * 8,
         scratch_shapes=[
             pltpu.SMEM((2, 2, 128), jnp.int32),
             pltpu.SMEM((RECEPTORS,), jnp.int32),
@@ -422,7 +446,9 @@
             pltpu.VMEM((PERIODS, PERIODS), F32),
             pltpu.VMEM((64, 64), F32),
             pltpu.VMEM((128, 1024), F32),
-            pltpu.SemaphoreType.DMA((8,)),
+            pltpu.SemaphoreType.DMA((10,)),
+            pltpu.SMEM((2 * RECEPTORS,), jnp.int32),
+            pltpu.VMEM((RECEPTORS, 2, WINDOW, 8, 128), F32),
             pltpu.VMEM((ROWS, 8, 128), F32),
             pltpu.VMEM((RECEPTORS, 128), F32),
             pltpu.VMEM((STRIPS, 2 * PERIODS, 128), F32),
@@ -463,16 +489,17 @@
             jax.ShapeDtypeStruct((SUM_ROWS, 8, 128), F32),
             jax.ShapeDtypeStruct((1, RECEPTORS), F32),
         ),
-        in_specs=[hbm, hbm, pl.BlockSpec(memory_space=pl.ANY), vmem, vmem],
-        out_specs=(vmem, vmem, vmem),
+        in_specs=[pl.BlockSpec(memory_space=pl.ANY)] * 3 + [vmem] * 4,
+        input_output_aliases={5: 0, 6: 1},
+        out_specs=(vmem, vmem, hbm),
         scratch_shapes=[
             pltpu.SMEM((2, 2, 128), jnp.int32),
             pltpu.SMEM((RECEPTORS,), jnp.int32),
             pltpu.SMEM((RECEPTORS,), F32),
-            pltpu.SemaphoreType.DMA((3,)),
+            pltpu.SemaphoreType.DMA((4,)),
         ],
         compiler_params=pltpu.CompilerParams(vmem_limit_bytes=VMEM_LIMIT),
-    )(in_hbm(slots), in_hbm(offset), misfit_row.reshape(RECEPTORS), packed, misfit_row)
+    )(slots_near, starts_near, misfit_row.reshape(RECEPTORS), packed, misfit_row, clear_one, clear_two)
     piece = (HALF, 8, 128)
     shape = (TILES // 2 + 1, 2, PERIODS, 8, 128)
     gradient = pl.pallas_call(

time: 44.3 us -> 43.2 us (0.975)
  Pallas kernels: 42.9 us -> 41.9 us
    pallas_call x1, Pallas kernels: 3.18 us -> 2.44 us  [shards(): pl.pallas_call(adjoint_kernel, name='adjoint', out_shape=(jax.ShapeDtypeS...]
where the time goes in v4:
time: 43.2 us
  Pallas kernels  41.9 us (97%)
  between operations  0.66 us (2%)
  local copies, waits for them, and re-layouts  0.63 us (1%)
    pallas_call x1, Pallas kernels, shards(): pl.pallas_call(forward_kernel, name='forward', out_shape=(jax.ShapeDtypeS...  27.2 us
    pallas_call x1, Pallas kernels, shards(): pl.pallas_call(scatter_kernel, name='scatter', out_shape=jax.ShapeDtypeSt...  12.3 us
    pallas_call x1, Pallas kernels, shards(): pl.pallas_call(adjoint_kernel, name='adjoint', out_shape=(jax.ShapeDtypeS...  2.44 us

profile of v4, /device:TPU:1, one launch (start us, length us, event | category | flops | bytes accessed | tf_op | source)
XLA Modules:
  0.0 43.2 jit_solution(9787052516432238646)
XLA Ops:
  0.6 27.2 %forward.1 = (f32[1,256]{1,0:T(1,128)S(1)}, f32[128,128]{1,0:T(8,128)S(1)}, f32[2,64,128]{2,1,0:T(8,128)S(1)}, bf16[256,2,8,8,128]{4,3,2,1,0:T(8,128)(2,1)S(1)},...) custom-call(s32[2,2,128]{2,1,0:T(2,128)} %bitcast.14, ...), custom_call_target="tpu_custom_call" | custom-call | tf_op jit(solution)/shard_map/forward/pallas_call | solution.py:425
  27.8 2.4 %adjoint.1 = (f32[640,8,128]{2,1,0:T(8,128)S(1)}, f32[640,8,128]{2,1,0:T(8,128)S(1)}, f32[1,256]{1,0:T(1,128)}) custom-call(s32[2,2,128]{2,1,0:T(2,128)S(1)} %get-tuple-element.13.slots_hbm, s32[256]{0:T(256)S(1)} %get-tuple-element.14.starts_hbm, f32[256]{0:T(256)S(1)} %bitcast.12, ...), custom_call_target="tpu_custom_call", output_to_operand_aliasing={{0}: (5, {}), {1}: (6, {})} | custom-call | tf_op jit(solution)/shard_map/adjoint/pallas_call | solution.py:484
  30.2 12.3 %scatter.1 = f32[64,2,128]{2,1,0:T(2,128)S(1)} custom-call(f32[5,2,64,8,128]{4,3,2,1,0:T(8,128)S(1)} %bitcast.10, f32[5,2,64,8,128]{4,3,2,1,0:T(8,128)S(1)} %bitcast.11, f32[128,128]{1,0:T(8,128)S(1)} %get-tuple-element.21.prior, f32[2,64,128]{2,1,0:T(8,128)S(1)} %get-tuple-element.22.lat), custom_call_target="tpu_custom_call" | custom-call | tf_op jit(solution)/shard_map/scatter/pallas_call | solution.py:505
  42.5 0.6 %copy.17 = f32[64,2,128]{2,1,0:T(2,128)} copy(f32[64,2,128]{2,1,0:T(2,128)S(1)} %scatter.1) | data formatting | bytes 131072

commit v5 on v4

--- a/solution.py
+++ b/solution.py
@@ -23,7 +23,7 @@
 RECEPTORS = 256
 STRIPS = 8
 GROUP = 8
-UNROLL = 8
+UNROLL = 16
 Z_NEAR = (2, 6, 1, 7)
 Z_FAR = (4, 3, 5)
 SENT_ROWS = 60 * 8 + 16
@@ -279,8 +279,6 @@
     prior_out[...] = jnp.dot(time_both, lon_done, precision=HIGHEST, preferred_element_type=F32)
 
     mine.wait()
-    sent = strip.at[pl.ds(0, SENT_ROWS)]
-    copy_to(sent, sent, send_sem, near_sem, partner).wait_send()
     others = shares.at[pl.ds(0, STRIPS - 1), :]
     copy_to(others, others, s_send, s_recv, partner).wait()
     predicted = jnp.sum(shares[...], axis=0, keepdims=True)
@@ -288,6 +286,8 @@
     for g in range(4):
         variance += jnp.where(group[...] == g, group_var[g], 0.0)
     misfit_out[...] = (predicted - observed[...]) / variance
+    sent = strip.at[pl.ds(0, SENT_ROWS)]
+    copy_to(sent, sent, send_sem, near_sem, partner).wait_send()
 
 
 def adjoint_kernel(
@@ -404,8 +404,6 @@
             send(17, b_sum.at[e - 1, :, mine, :], b_last.at[e - 1, :, mine, :], (rec_of(x + e, y, c), z))
         else:
             done[second_half] = b_total
-    sent = total.at[pl.ds(0, 4), :, pl.ds(0, 62), :, :]
-    copy_to(sent, sent, send_sem, recv_sem.at[0], partner).wait_send()
     arrived(16, a_last.at[:, :, mine, :])
     out[first_half] = (
         done[first_half, mine, :] + a_last[0, :, mine, :] + a_last[1, :, mine, :] + a_last[2, :, mine, :]
@@ -414,6 +412,8 @@
     out[second_half] = (
         done[second_half, mine, :] + b_last[0, :, mine, :] + b_last[1, :, mine, :] + b_last[2, :, mine, :]
     )
+    sent = total.at[pl.ds(0, 4), :, pl.ds(0, 62), :, :]
+    copy_to(sent, sent, send_sem, recv_sem.at[0], partner).wait_send()
 
 
 def shards(

time: 43.2 us -> 43.3 us (level)
  no operation moved by 1% of the time
where the time goes in v5:
time: 43.3 us; the launch traced here: 43.2 us
  Pallas kernels  41.9 us (97%)
  between operations  0.66 us (2%)
  local copies, waits for them, and re-layouts  0.63 us (1%)
    pallas_call x1, Pallas kernels, shards(): pl.pallas_call(forward_kernel, name='forward', out_shape=(jax.ShapeDtypeS...  27.1 us
    pallas_call x1, Pallas kernels, shards(): pl.pallas_call(scatter_kernel, name='scatter', out_shape=jax.ShapeDtypeSt...  12.4 us
    pallas_call x1, Pallas kernels, shards(): pl.pallas_call(adjoint_kernel, name='adjoint', out_shape=(jax.ShapeDtypeS...  2.41 us

profile of v5, /device:TPU:1, one launch (start us, length us, event | category | flops | bytes accessed | tf_op | source)
XLA Modules:
  0.0 43.2 jit_solution(752266406054944881)
XLA Ops:
  0.6 27.1 %forward.1 = (f32[1,256]{1,0:T(1,128)S(1)}, f32[128,128]{1,0:T(8,128)S(1)}, f32[2,64,128]{2,1,0:T(8,128)S(1)}, bf16[256,2,8,8,128]{4,3,2,1,0:T(8,128)(2,1)S(1)},...) custom-call(s32[2,2,128]{2,1,0:T(2,128)} %bitcast.14, ...), custom_call_target="tpu_custom_call" | custom-call | tf_op jit(solution)/shard_map/forward/pallas_call | solution.py:425
  27.8 2.4 %adjoint.1 = (f32[640,8,128]{2,1,0:T(8,128)S(1)}, f32[640,8,128]{2,1,0:T(8,128)S(1)}, f32[1,256]{1,0:T(1,128)}) custom-call(s32[2,2,128]{2,1,0:T(2,128)S(1)} %get-tuple-element.13.slots_hbm, s32[256]{0:T(256)S(1)} %get-tuple-element.14.starts_hbm, f32[256]{0:T(256)S(1)} %bitcast.12, ...), custom_call_target="tpu_custom_call", output_to_operand_aliasing={{0}: (5, {}), {1}: (6, {})} | custom-call | tf_op jit(solution)/shard_map/adjoint/pallas_call | solution.py:484
  30.2 12.4 %scatter.1 = f32[64,2,128]{2,1,0:T(2,128)S(1)} custom-call(f32[5,2,64,8,128]{4,3,2,1,0:T(8,128)S(1)} %bitcast.10, f32[5,2,64,8,128]{4,3,2,1,0:T(8,128)S(1)} %bitcast.11, f32[128,128]{1,0:T(8,128)S(1)} %get-tuple-element.21.prior, f32[2,64,128]{2,1,0:T(8,128)S(1)} %get-tuple-element.22.lat), custom_call_target="tpu_custom_call" | custom-call | tf_op jit(solution)/shard_map/scatter/pallas_call | solution.py:505
  42.6 0.6 %copy.17 = f32[64,2,128]{2,1,0:T(2,128)} copy(f32[64,2,128]{2,1,0:T(2,128)S(1)} %scatter.1) | data formatting | bytes 131072

commit v6 on v4

--- a/solution.py
+++ b/solution.py
@@ -22,7 +22,7 @@
 SUM_ROWS = (TILES + 2) * PERIODS
 RECEPTORS = 256
 STRIPS = 8
-GROUP = 8
+GROUP = 16
 UNROLL = 8
 Z_NEAR = (2, 6, 1, 7)
 Z_FAR = (4, 3, 5)
@@ -255,7 +255,7 @@
         return carry
 
     for block in range(2):
-        lax.fori_loop(0, 128 // GROUP, functools.partial(group_sums, block), 0, unroll=2)
+        lax.fori_loop(0, 128 // GROUP, functools.partial(group_sums, block), 0)
     share = lax.dot_general(
         jnp.ones((8, 128), F32), sums[...], (((1,), (1,)), ((), ())), precision=HIGHEST, preferred_element_type=F32
     )

time: 43.2 us -> 43.3 us (level)
  no operation moved by 1% of the time
where the time goes in v6:
time: 43.3 us
  Pallas kernels  42 us (97%)
  between operations  0.66 us (2%)
  local copies, waits for them, and re-layouts  0.63 us (1%)
    pallas_call x1, Pallas kernels, shards(): pl.pallas_call(forward_kernel, name='forward', out_shape=(jax.ShapeDtypeS...  27.1 us
    pallas_call x1, Pallas kernels, shards(): pl.pallas_call(scatter_kernel, name='scatter', out_shape=jax.ShapeDtypeSt...  12.4 us
    pallas_call x1, Pallas kernels, shards(): pl.pallas_call(adjoint_kernel, name='adjoint', out_shape=(jax.ShapeDtypeS...  2.45 us

profile of v6, /device:TPU:1, one launch (start us, length us, event | category | flops | bytes accessed | tf_op | source)
XLA Modules:
  0.0 43.3 jit_solution(12579779557488558956)
XLA Ops:
  0.6 27.1 %forward.1 = (f32[1,256]{1,0:T(1,128)S(1)}, f32[128,128]{1,0:T(8,128)S(1)}, f32[2,64,128]{2,1,0:T(8,128)S(1)}, bf16[256,2,8,8,128]{4,3,2,1,0:T(8,128)(2,1)S(1)},...) custom-call(s32[2,2,128]{2,1,0:T(2,128)} %bitcast.14, ...), custom_call_target="tpu_custom_call" | custom-call | tf_op jit(solution)/shard_map/forward/pallas_call | solution.py:425
  27.8 2.4 %adjoint.1 = (f32[640,8,128]{2,1,0:T(8,128)S(1)}, f32[640,8,128]{2,1,0:T(8,128)S(1)}, f32[1,256]{1,0:T(1,128)}) custom-call(s32[2,2,128]{2,1,0:T(2,128)S(1)} %get-tuple-element.13.slots_hbm, s32[256]{0:T(256)S(1)} %get-tuple-element.14.starts_hbm, f32[256]{0:T(256)S(1)} %bitcast.12, ...), custom_call_target="tpu_custom_call", output_to_operand_aliasing={{0}: (5, {}), {1}: (6, {})} | custom-call | tf_op jit(solution)/shard_map/adjoint/pallas_call | solution.py:484
  30.2 12.4 %scatter.1 = f32[64,2,128]{2,1,0:T(2,128)S(1)} custom-call(f32[5,2,64,8,128]{4,3,2,1,0:T(8,128)S(1)} %bitcast.10, f32[5,2,64,8,128]{4,3,2,1,0:T(8,128)S(1)} %bitcast.11, f32[128,128]{1,0:T(8,128)S(1)} %get-tuple-element.21.prior, f32[2,64,128]{2,1,0:T(8,128)S(1)} %get-tuple-element.22.lat), custom_call_target="tpu_custom_call" | custom-call | tf_op jit(solution)/shard_map/scatter/pallas_call | solution.py:505
  42.7 0.6 %copy.17 = f32[64,2,128]{2,1,0:T(2,128)} copy(f32[64,2,128]{2,1,0:T(2,128)S(1)} %scatter.1) | data formatting | bytes 131072
